TPU v7x, 128 devices: a whole 4x4x4 slice. The times are simulated.
128 devices in a mesh: ctx: 8 (over z, x_hi), fsdp: 16 (over y, x_lo, core).
Axes of the slice: x: 4 (x_hi: 2, x_lo: 2; x = x_hi * 2 + x_lo), y: 4, z: 4, core: 2. Of those that a mesh axis runs over, the one named last changes fastest.
Arguments:
- queries: bfloat16 [16, 2048, 2048], P('fsdp', 'ctx'), may hold values from -36 to 36
- keys: bfloat16 [16, 2048, 512], P('fsdp', 'ctx'), may hold values from -6 to 6
- values: bfloat16 [16, 2048, 512], P('fsdp', 'ctx'), may hold values from -6 to 6
- resid: bfloat16 [16, 2048, 2048], P('fsdp', 'ctx'), may hold values from -6 to 6
- grad_out: bfloat16 [16, 2048, 2048], P('fsdp', 'ctx'), may hold values from -8 to 8
- w_out: bfloat16 [2048, 2048], P(None, 'fsdp'), may hold values from -0.125 to 0.125
- block_list: int32 [16, 8], P('ctx'), may hold values from 0 to 15, as said below
- block_count: int32 [16], P('ctx'), may hold values from 1 to 8, as said below
Outputs:
- mixed: bfloat16 [16, 2048, 2048], P('fsdp', 'ctx')
- query_grad: bfloat16 [16, 2048, 2048], P('fsdp', 'ctx')
- key_grad: bfloat16 [16, 2048, 512], P('fsdp', 'ctx')
- value_grad: bfloat16 [16, 2048, 512], P('fsdp', 'ctx')
- proj_grad: float32 [2048, 2048], P('ctx', 'fsdp')
Inputs may be any that keep to these rules, and one draw needn't show every extreme that they name: `block_list`: row r lists the key blocks of query block r within its sequence: entry 0 is r itself; entries 1 to block_count[r] - 1 are distinct blocks before r; entries from block_count[r] on are ignored and hold r or earlier blocks. block_count[r] is at most min(r + 1, 8); the last query block has exactly 8.
All inputs are finite; a program needn't handle non-finite values.
Results may differ from a plain program's by a relative error of at most 0.025.
Values may be sent and summed in bfloat16 or wider, within the bound.
A program may use at most 192 MiB of HBM per device.

v0:
```python
import math

import jax
import jax.numpy as jnp
from jax import lax
from jax.sharding import PartitionSpec as P

QUERY_HEADS = 16
KEY_VALUE_HEADS = 4
HEAD_DIM = 128
BLOCK_SIZE = 128
KEY_SLOTS = 8


def score_mask(first_row, listed_blocks, live_count):
    query_pos = first_row + jnp.arange(BLOCK_SIZE, dtype=jnp.int32)
    key_pos = listed_blocks[:, None] * BLOCK_SIZE + jnp.arange(BLOCK_SIZE, dtype=jnp.int32)[None, :]
    slot_live = jnp.arange(KEY_SLOTS, dtype=jnp.int32) < live_count
    return (key_pos[None, :, :] <= query_pos[:, None, None]) & slot_live[None, :, None]


def block_weights(query_blk, key_sel, allowed):
    scale = 1.0 / math.sqrt(HEAD_DIM)
    scores = (
        jnp.einsum("qgrd,sbgd->grqsb", query_blk, key_sel, preferred_element_type=jnp.float32)
        * scale
    )
    scores = jnp.where(allowed[None, None], scores, jnp.float32(-1e30))
    top = jnp.max(scores, axis=(3, 4), keepdims=True)
    expon = jnp.exp(scores - top)
    probs = expon / jnp.sum(expon, axis=(3, 4), keepdims=True)
    return (probs, probs.astype(jnp.bfloat16))


def local(queries, keys, values, resid, grad_out, w_out, block_list, block_count):
    scale = 1.0 / math.sqrt(HEAD_DIM)
    query_groups = QUERY_HEADS // KEY_VALUE_HEADS
    seq_rows = queries.shape[1]
    device_local_blocks = seq_rows // BLOCK_SIZE
    first_block = lax.axis_index("ctx") * device_local_blocks
    block_pos = first_block + jnp.arange(device_local_blocks, dtype=jnp.int32)
    complete_keys, complete_values = (
        lax.all_gather(keys, "ctx", axis=1, tiled=True),
        lax.all_gather(values, "ctx", axis=1, tiled=True),
    )
    block_total = complete_keys.shape[1] // BLOCK_SIZE
    blocked_keys = complete_keys[0].reshape(block_total, BLOCK_SIZE, KEY_VALUE_HEADS, HEAD_DIM)
    blocked_values = complete_values[0].reshape(block_total, BLOCK_SIZE, KEY_VALUE_HEADS, HEAD_DIM)
    blocked_queries = queries[0].reshape(
        device_local_blocks, BLOCK_SIZE, KEY_VALUE_HEADS, query_groups, HEAD_DIM
    )

    def forward_block(operands):
        query_blk, listed_blocks, live_count, position = operands
        allowed = score_mask(position * BLOCK_SIZE, listed_blocks, live_count)
        key_sel = jnp.take(blocked_keys, listed_blocks, axis=0)
        value_sel = jnp.take(blocked_values, listed_blocks, axis=0)
        probs, probs_b = block_weights(query_blk, key_sel, allowed)
        attended = jnp.einsum(
            "grqsb,sbgd->qgrd", probs_b, value_sel, preferred_element_type=jnp.float32
        )
        return attended.astype(jnp.bfloat16)

    out_blocks = lax.map(forward_block, (blocked_queries, block_list, block_count, block_pos))
    out_rows = out_blocks.reshape(seq_rows, QUERY_HEADS * HEAD_DIM)
    grad_rows = grad_out[0]
    w_whole = lax.all_gather(w_out, "fsdp", axis=1, tiled=True)
    projected = jnp.dot(out_rows, w_whole, preferred_element_type=jnp.float32)
    attended_gradient = lax.dot_general(
        grad_rows, w_whole, (((1,), (1,)), ((), ())), preferred_element_type=jnp.float32
    )
    mixed = (resid[0].astype(jnp.float32) + projected).astype(jnp.bfloat16)
    output_grad_blocks = attended_gradient.astype(jnp.bfloat16).reshape(
        device_local_blocks, BLOCK_SIZE, KEY_VALUE_HEADS, query_groups, HEAD_DIM
    )

    def backward_block(operands):
        query_blk, out_blk, dout_blk, listed_blocks, live_count, position = operands
        allowed = score_mask(position * BLOCK_SIZE, listed_blocks, live_count)
        key_sel = jnp.take(blocked_keys, listed_blocks, axis=0)
        value_sel = jnp.take(blocked_values, listed_blocks, axis=0)
        probs, probs_b = block_weights(query_blk, key_sel, allowed)
        value_part = jnp.einsum(
            "grqsb,qgrd->sbgd", probs_b, dout_blk, preferred_element_type=jnp.float32
        )
        prob_grads = jnp.einsum(
            "qgrd,sbgd->grqsb", dout_blk, value_sel, preferred_element_type=jnp.float32
        )
        row_dot = jnp.sum(dout_blk.astype(jnp.float32) * out_blk.astype(jnp.float32), axis=-1)
        row_dot = jnp.transpose(row_dot, (1, 2, 0))[:, :, :, None, None]
        score_grads = (probs * (prob_grads - row_dot) * scale).astype(jnp.bfloat16)
        query_part = jnp.einsum(
            "grqsb,sbgd->qgrd", score_grads, key_sel, preferred_element_type=jnp.float32
        ).astype(jnp.bfloat16)
        key_part = jnp.einsum(
            "grqsb,qgrd->sbgd", score_grads, query_blk, preferred_element_type=jnp.float32
        )
        return (query_part, key_part, value_part)

    query_parts, key_fragments, value_fragments = lax.map(
        backward_block,
        (blocked_queries, out_blocks, output_grad_blocks, block_list, block_count, block_pos),
    )
    listed_all = block_list.reshape(-1)
    key_holder = (
        jnp.zeros((block_total, BLOCK_SIZE, KEY_VALUE_HEADS * HEAD_DIM), jnp.float32)
        .at[listed_all]
        .add(
            key_fragments.reshape(
                device_local_blocks * KEY_SLOTS, BLOCK_SIZE, KEY_VALUE_HEADS * HEAD_DIM
            )
        )
    )
    value_holder = (
        jnp.zeros((block_total, BLOCK_SIZE, KEY_VALUE_HEADS * HEAD_DIM), jnp.float32)
        .at[listed_all]
        .add(
            value_fragments.reshape(
                device_local_blocks * KEY_SLOTS, BLOCK_SIZE, KEY_VALUE_HEADS * HEAD_DIM
            )
        )
    )
    key_sum, value_sum = (
        lax.psum_scatter(
            key_holder.reshape(1, block_total * BLOCK_SIZE, KEY_VALUE_HEADS * HEAD_DIM).astype(
                jnp.bfloat16
            ),
            "ctx",
            scatter_dimension=1,
            tiled=True,
        ).astype(jnp.float32),
        lax.psum_scatter(
            value_holder.reshape(1, block_total * BLOCK_SIZE, KEY_VALUE_HEADS * HEAD_DIM).astype(
                jnp.bfloat16
            ),
            "ctx",
            scatter_dimension=1,
            tiled=True,
        ).astype(jnp.float32),
    )
    feature_share = lax.psum_scatter(
        lax.dot_general(
            grad_rows, out_rows, (((0,), (0,)), ((), ())), preferred_element_type=jnp.float32
        ).astype(jnp.bfloat16),
        "fsdp",
        scatter_dimension=0,
        tiled=True,
    )
    proj_grad = (
        lax.psum_scatter(feature_share, "ctx", scatter_dimension=1, tiled=True)
        .astype(jnp.float32)
        .T
    )
    query_grad = query_parts.reshape(1, seq_rows, QUERY_HEADS * HEAD_DIM)
    return (
        mixed[None],
        query_grad,
        key_sum.astype(jnp.bfloat16),
        value_sum.astype(jnp.bfloat16),
        proj_grad,
    )


def solution(mesh):
    in_specs = (
        P("fsdp", "ctx", None),
        P("fsdp", "ctx", None),
        P("fsdp", "ctx", None),
        P("fsdp", "ctx", None),
        P("fsdp", "ctx", None),
        P(None, "fsdp"),
        P("ctx", None),
        P("ctx"),
    )
    out_specs = (
        P("fsdp", "ctx", None),
        P("fsdp", "ctx", None),
        P("fsdp", "ctx", None),
        P("fsdp", "ctx", None),
        P("ctx", "fsdp"),
    )
    return jax.shard_map(local, mesh=mesh, in_specs=in_specs, out_specs=out_specs, check_vma=False)
```

profile of v0, /device:TPU:0, one launch (start us, length us, event | category | flops | bytes accessed | tf_op | source)
XLA Modules:
  0.0 542.3 jit_solution(563951076636998370)
XLA Ops:
  12.5 54.5 %all-gather.4.cloned.1.call-done = bf16[1,2048,512]{2,1,0:T(8,128)(2,1)} async-done(((bf16[1,256,512]{2,1,0:T(8,128)(2,1)}), bf16[1,2048,512]{2,1,0:T(8,128)(2,1)}) %all-gather.4.cloned.1.call-update) | async-done | bytes 2097168 | tf_op jit(solution)/shard_map/all_gather | solution.py:44
  67.0 4.0 reshape_squeeze.9
  71.0 50.3 %all-gather.6.cloned.1.call-done = bf16[1,2048,512]{2,1,0:T(8,128)(2,1)} async-done(((bf16[1,256,512]{2,1,0:T(8,128)(2,1)}), bf16[1,2048,512]{2,1,0:T(8,128)(2,1)}) %all-gather.6.cloned.1.call-update) | async-done | bytes 2097168 | tf_op jit(solution)/shard_map/all_gather | solution.py:43
  121.3 4.0 reshape_squeeze.10
  125.3 35.7 %while.24 = (s32[]{:T(128)}, bf16[2,128,4,4,128]{1,4,3,2,0:T(8,128)(2,1)}, s32[2,8]{1,0:T(2,128)S(1)}, bf16[16,128,4,128]{3,2,1,0:T(4,128)(2,1)}, s32[2]{0:T(128...) while((s32[]{:T(128)}, ...), condition=%wide.region_3.5_spmd, body=%wide.region_0.4_spmd.sunk | while | flops 1100478720 | bytes 45667840 | solution.py:64
  146.1 3.2 gather_fusion.1
  163.9 5.6 %convert_bitcast_fusion = bf16[2048,2048]{0,1:T(8,128)(2,1)} fusion(bf16[256,2048]{1,0:T(8,128)(2,1)S(1)} %reshape.176, bf16[1,256,2048]{2,1,0:T(8,128)(2,1)S(1)} %copy-done), kind=kOutput, calls=%fused_computation.87 | convolution fusion | flops 2151677952 | bytes 10485760 | tf_op jit(solution)/shard_map/dot_general | solution.py:142
  169.5 12.3 %copy.122 = bf16[2048,2048]{1,0:T(8,128)(2,1)} copy(bf16[2048,2048]{0,1:T(8,128)(2,1)} %convert_bitcast_fusion) | data formatting | bytes 16777216
  182.6 5.7 %convolution_convert_fusion = bf16[256,2048]{1,0:T(8,128)(2,1)S(1)} fusion(bf16[2048,2048]{1,0:T(8,128)(2,1)} %all-gather.8.cloned.1.call-done, bf16[1,256,2048]{2,1,0:T(8,128)(2,1)S(1)} %copy-done), kind=kOutput, calls=%fused_computation.90 | convolution fusion | flops 2148007936 | bytes 10485760 | tf_op jit(solution)/shard_map/dot_general | solution.py:69
  189.9 91.2 %reduce-scatter.13.cloned.1.call-done = bf16[128,2048]{1,0:T(8,128)(2,1)} async-done(((bf16[2048,2048]{1,0:T(8,128)(2,1)}), bf16[128,2048]{1,0:T(8,128)(2,1)}) %reduce-scatter.13.cloned.1.call-update) | async-done | bytes 524304
  283.2 78.1 %while.25 = (s32[]{:T(128)}, bf16[2,128,4,4,128]{4,3,2,1,0:T(4,128)(2,1)}, f32[2,8,128,4,128]{2,4,3,1,0:T(8,128)}, f32[2,8,128,4,128]{2,4,3,1,0:T(8,128)}, s32[2...) while((s32[]{:T(128)}, ...), condition=%wide.region_8.10_spmd, body=%wide.region_4.9_spmd.sunk | while | flops 2728915200 | bytes 224614144 | solution.py:100
  302.3 3.4 fusion.109
  310.0 5.0 fusion.111
  341.4 3.4 fusion.109
  349.1 5.0 fusion.111
  361.3 5.4 copy.85
  369.2 9.4 %scatter_fusion = f32[16,128,512]{2,1,0:T(8,128)} fusion(f32[16,128,512]{2,1,0:T(8,128)} %broadcast.137.clone, s32[16]{0:T(128)S(1)} %copy-done.17, f32[16,128,512]{2,1,0:T(8,128)} %copy.85), kind=kCustom, calls=%fused_computation.4 | custom fusion | flops 1048576 | bytes 12582976 | tf_op jit(solution)/shard_map/scatter-add | solution.py:108
  378.6 3.8 convert_element_type.85
  382.5 5.4 copy.87
  390.3 9.4 %scatter_fusion.1 = f32[16,128,512]{2,1,0:T(8,128)} fusion(f32[16,128,512]{2,1,0:T(8,128)} %broadcast.137.clone.1, s32[16]{0:T(128)S(1)} %copy-done.17, f32[16,128,512]{2,1,0:T(8,128)} %copy.87), kind=kCustom, calls=%fused_computation.5 | custom fusion | flops 1048576 | bytes 12582976 | tf_op jit(solution)/shard_map/scatter-add | solution.py:117
  399.8 4.0 convert_element_type.87
  405.4 7.0 %fusion.64 = bf16[1,256,2048]{2,1,0:T(8,128)(2,1)} fusion(bf16[256,2048]{1,0:T(8,128)(2,1)S(1)} %copy-done.10, bf16[2048,2048]{1,0:T(8,128)(2,1)} %all-gather.8.cloned.1.call-done, bf16[1,256,2048]{2,1,0:T(8,128)(2,1)} %param.17), kind=kOutput, calls=%fused_computation.91 | convolution fusion | flops 2149056512 | bytes 11534336 | tf_op jit(solution)/shard_map/dot_general | solution.py:68
  413.9 42.9 %reduce-scatter.7.cloned.1.call-done = bf16[1,256,512]{2,1,0:T(8,128)(2,1)} async-done(((bf16[1,2048,512]{2,1,0:T(8,128)(2,1)}), bf16[1,256,512]{2,1,0:T(8,128)(2,1)}) %reduce-scatter.7.cloned.1.call-update) | async-done | bytes 262160 | tf_op jit(solution)/shard_map/reduce_scatter | solution.py:124
  456.7 78.7 %reduce-scatter.9.cloned.1.call-done = bf16[1,256,512]{2,1,0:T(8,128)(2,1)} async-done(((bf16[1,2048,512]{2,1,0:T(8,128)(2,1)}), bf16[1,256,512]{2,1,0:T(8,128)(2,1)}) %reduce-scatter.9.cloned.1.call-update) | async-done | bytes 262160 | tf_op jit(solution)/shard_map/reduce_scatter | solution.py:132
  (170 shorter events, 111.2 us)
Async XLA Ops:
  7.2 156.7 %copy-start = (bf16[1,256,2048]{2,1,0:T(8,128)(2,1)S(1)}, bf16[1,256,2048]{2,1,0:T(8,128)(2,1)}, u32[]{:S(2)}) copy-start(bf16[1,256,2048]{2,1,0:T(8,128)(2,1)} %param.18) | copy-start | bytes 3145732
  7.2 118.1 %copy-start.16 = (s32[2,8]{1,0:T(2,128)S(1)}, s32[2,8]{1,0:T(2,128)}, u32[]{:S(2)}) copy-start(s32[2,8]{1,0:T(2,128)} %param.20) | copy-start | bytes 196
  7.2 118.1 %copy-start.18 = (s32[2]{0:T(128)S(1)}, s32[2]{0:T(128)}, u32[]{:S(2)}) copy-start(s32[2]{0:T(128)} %param.21) | copy-start | bytes 28
  7.2 59.8 %all-gather.4.cloned.1.call-start = ((), (), s32[]{:S(2)}) async-start(), calls=%async_computation.4 | async-start | bytes 2359296 | tf_op jit(solution)/shard_map/all_gather | solution.py:44
  7.9 113.4 %all-gather.6.cloned.1.call-start = ((), (), s32[]{:S(2)}) async-start(), calls=%async_computation.5 | async-start | bytes 2359296 | tf_op jit(solution)/shard_map/all_gather | solution.py:43
  8.7 173.9 %all-gather.8.cloned.1.call-start = ((), (), s32[]{:S(2)}) async-start(), calls=%async_computation.6 | async-start | bytes 8912896 | tf_op jit(solution)/shard_map/all_gather | solution.py:67
  9.4 271.6 %reduce-scatter.13.cloned.1.call-start = ((), (), s32[]{:S(2)}) async-start(), calls=%async_computation.10 | async-start | bytes 8912896
  153.1 4.3 copy-start.7
  163.9 18.0 %copy-start.9 = (bf16[256,2048]{1,0:T(8,128)(2,1)}, bf16[256,2048]{1,0:T(8,128)(2,1)S(1)}, u32[]{:S(2)}) copy-start(bf16[256,2048]{1,0:T(8,128)(2,1)S(1)} %reshape.176) | copy-start | bytes 3145732
  181.9 230.5 %reduce-scatter.11.cloned.1.call-start = ((), (), s32[]{:S(2)}) async-start(), calls=%async_computation.9 | async-start | bytes 589824 | tf_op jit(solution)/shard_map/reduce_scatter | solution.py:150
  283.1 173.6 %reduce-scatter.7.cloned.1.call-start = ((), (), s32[]{:S(2)}) async-start(), calls=%async_computation.7 | async-start | bytes 2359296 | tf_op jit(solution)/shard_map/reduce_scatter | solution.py:124
  297.9 4.4 copy-start.6
  300.6 5.2 copy-start.2
  310.0 5.0 copy-start.4
  310.0 5.0 copy-start.5
  337.0 4.4 copy-start.6
  339.6 5.2 copy-start.2
  349.1 5.0 copy-start.4
  349.1 5.0 copy-start.5
  361.3 7.9 %copy-start.17 = (s32[16]{0:T(128)S(1)}, s32[16]{0:T(128)}, u32[]{:S(2)}) copy-start(s32[16]{0:T(128)} %fusion.67) | copy-start | bytes 196
  382.4 153.0 %reduce-scatter.9.cloned.1.call-start = ((), (), s32[]{:S(2)}) async-start(), calls=%async_computation.8 | async-start | bytes 2359296 | tf_op jit(solution)/shard_map/reduce_scatter | solution.py:132
  390.3 13.4 %copy-start.15 = (bf16[2,128,4,4,128]{4,3,2,1,0:T(4,128)(2,1)S(1)}, bf16[2,128,4,4,128]{4,3,2,1,0:T(4,128)(2,1)}, u32[]{:S(2)}) copy-start(bf16[2,128,4,4,128]{4,3,2,1,0:T(4,128)(2,1)} %get-tuple-element.113) | copy-start | bytes 3145732
  399.7 5.6 %copy-start.10 = (bf16[256,2048]{1,0:T(8,128)(2,1)S(1)}, bf16[256,2048]{1,0:T(8,128)(2,1)}, u32[]{:S(2)}) copy-start(bf16[256,2048]{1,0:T(8,128)(2,1)} %copy-done.9) | copy-start | bytes 3145732
  403.7 131.7 %copy-start.1 = (bf16[1,256,2048]{2,1,0:T(8,128)(2,1)S(1)}, bf16[1,256,2048]{2,1,0:T(8,128)(2,1)}, u32[]{:S(2)}) copy-start(bf16[1,256,2048]{2,1,0:T(8,128)(2,1)} %param.18) | copy-start | bytes 3145732
  (13 other events, 31.9 us)
Sparse Core Ops, SparseCore 0:
  10.4 56.5 all-gather.3
  69.4 51.8 all-gather.5
  123.0 58.0 all-gather.7
  183.3 97.6 reduce-scatter.12
  284.4 69.2 reduce-scatter.10
  382.6 74.1 reduce-scatter.6
  461.5 73.8 reduce-scatter.8
where the time goes:
time: 544 us; the launch traced here: 542 us
  waiting for transfers between devices  320 us (59%)
  local copies, waits for them, and re-layouts  103 us (19%)
  matrix products  55.3 us (10%)
  other arithmetic  46.2 us (8%)
  between operations  14.3 us (3%)
    unnamed x8, waiting for transfers between devices  93.3 us
    reduce_scatter x1, waiting for transfers between devices, local(): lax.psum_scatter(value_holder.reshape(1, block_total * BLOCK_SIZE, KEY_VA...  78.7 us
    all_gather x1, waiting for transfers between devices, local(): lax.all_gather(values, 'ctx', axis=1, tiled=True)  54.5 us
    all_gather x1, waiting for transfers between devices, local(): lax.all_gather(keys, 'ctx', axis=1, tiled=True)  50.3 us
    reduce_scatter x1, waiting for transfers between devices, local(): lax.psum_scatter(key_holder.reshape(1, block_total * BLOCK_SIZE, KEY_VALU...  42.9 us
    while x44, local copies, waits for them, and re-layouts  16.2 us
    unnamed x18, local copies, waits for them, and re-layouts  14.4 us
  transfers between devices with their start and end apart: 7, of which 5 were waited for; matrix products, arithmetic and copies ran while one was open for 34% of the time, Pallas kernels for 0%

commit v1 on v0

v1 whole, which is shorter than its diff:
```python
import math

import jax
import jax.numpy as jnp
from jax import lax
from jax.experimental import pallas as pl
from jax.experimental.pallas import tpu as pltpu
from jax.sharding import PartitionSpec as P

QUERY_HEADS = 16
KV_HEADS = 4
GROUP = QUERY_HEADS // KV_HEADS
HEAD_DIM = 128
BLOCK = 128
SLOTS = 8
SCALE = 1.0 / math.sqrt(HEAD_DIM)
BF16 = jnp.bfloat16
F32 = jnp.float32
MESH = pl.DeviceIdType.MESH


def dot(a, b, ca, cb):
    return lax.dot_general(a, b, (((ca,), (cb,)), ((), ())), preferred_element_type=F32)


def stack_heads(x):
    return jnp.concatenate(
        [x[:, h * HEAD_DIM : (h + 1) * HEAD_DIM] for h in range(GROUP)], axis=0
    )


def attention_kernel(
    list_ref, count_ref, q_ref, do_ref, k_ref, v_ref, att_ref, dq_ref, dk_ref, dv_ref, dk_acc, dv_acc
):
    i = pl.program_id(1)
    cols = GROUP * BLOCK

    @pl.when(i == 0)
    def _():
        dk_acc[...] = jnp.zeros_like(dk_acc)
        dv_acc[...] = jnp.zeros_like(dv_acc)

    q4 = stack_heads(q_ref[...])
    do4 = stack_heads(do_ref[...])
    live = count_ref[i]
    rows = [pl.ds(pl.multiple_of(list_ref[i, j] * BLOCK, BLOCK), BLOCK) for j in range(SLOTS)]
    k_sel = jnp.concatenate([k_ref[0, r, :] for r in rows], axis=0)
    v_sel = jnp.concatenate([v_ref[0, r, :] for r in rows], axis=0)
    s = dot(k_sel, q4, 1, 1)
    key_pos = lax.broadcasted_iota(jnp.int32, (BLOCK, cols), 0)
    query_pos = lax.broadcasted_iota(jnp.int32, (BLOCK, cols), 1) % BLOCK
    parts = [jnp.where(key_pos <= query_pos, s[:BLOCK], -1e30)]
    for j in range(1, SLOTS):
        bias = jnp.where(j < live, 0.0, -1e30).astype(F32)
        parts.append(s[j * BLOCK : (j + 1) * BLOCK] + bias)
    s = jnp.concatenate(parts, axis=0)
    top = jnp.max(s, axis=0, keepdims=True)
    e = jnp.exp((s - top) * SCALE)
    p = e * (1.0 / jnp.sum(e, axis=0, keepdims=True))
    pb = p.astype(BF16)
    o_t = dot(v_sel, pb, 0, 0)
    o4 = o_t.T.astype(BF16)
    row_dot = jnp.sum(o4.astype(F32) * do4.astype(F32), axis=1, keepdims=True)
    row_dot = jnp.broadcast_to(row_dot, (cols, HEAD_DIM)).T[:1]
    dp = dot(v_sel, do4, 1, 1)
    ds = (p * (dp - row_dot) * SCALE).astype(BF16)
    dq4 = dot(k_sel, ds, 0, 0).T.astype(BF16)
    dk_sel = dot(ds, q4, 1, 0)
    dv_sel = dot(pb, do4, 1, 0)
    for h in range(GROUP):
        att_ref[:, h * HEAD_DIM : (h + 1) * HEAD_DIM] = o4[h * BLOCK : (h + 1) * BLOCK]
        dq_ref[:, h * HEAD_DIM : (h + 1) * HEAD_DIM] = dq4[h * BLOCK : (h + 1) * BLOCK]
    for j in range(SLOTS):
        dk_acc[rows[j], :] += dk_sel[j * BLOCK : (j + 1) * BLOCK]
        dv_acc[rows[j], :] += dv_sel[j * BLOCK : (j + 1) * BLOCK]

    @pl.when(i == pl.num_programs(1) - 1)
    def _():
        dk_ref[0] = dk_acc[...].astype(BF16)
        dv_ref[0] = dv_acc[...].astype(BF16)


def attention(queries, datt, kv, block_list, block_count):
    rows, width = queries.shape
    seq = kv.shape[1]
    group_cols = GROUP * HEAD_DIM
    kv_cols = KV_HEADS * HEAD_DIM
    q_spec = pl.BlockSpec((BLOCK, group_cols), lambda g, i, *_: (i, g))

    def kv_spec(which):
        return pl.BlockSpec((1, seq, HEAD_DIM), lambda g, i, *_: (which, 0, g))

    out_spec = pl.BlockSpec((1, seq, HEAD_DIM), lambda g, i, *_: (0, 0, g))
    flops = 12 * rows * QUERY_HEADS * SLOTS * BLOCK * HEAD_DIM
    return pl.pallas_call(
        attention_kernel,
        grid_spec=pltpu.PrefetchScalarGridSpec(
            num_scalar_prefetch=2,
            grid=(KV_HEADS, rows // BLOCK),
            in_specs=[q_spec, q_spec, kv_spec(0), kv_spec(1)],
            out_specs=[q_spec, q_spec, out_spec, out_spec],
            scratch_shapes=[pltpu.VMEM((seq, HEAD_DIM), F32)] * 2,
        ),
        out_shape=[
            jax.ShapeDtypeStruct((rows, width), BF16),
            jax.ShapeDtypeStruct((rows, width), BF16),
            jax.ShapeDtypeStruct((1, seq, kv_cols), BF16),
            jax.ShapeDtypeStruct((1, seq, kv_cols), BF16),
        ],
        compiler_params=pltpu.CompilerParams(
            dimension_semantics=("arbitrary", "arbitrary"), vmem_limit_bytes=48 << 20
        ),
        cost_estimate=pl.CostEstimate(
            flops=flops, bytes_accessed=12 << 20, transcendentals=rows * QUERY_HEADS * SLOTS * BLOCK
        ),
        name="attention",
    )(block_list, block_count, queries, datt, kv, kv)


def mesh_spot():
    c, f = lax.axis_index("ctx"), lax.axis_index("fsdp")
    return c, f, c // 2, lax.rem(c, 2), f // 4, lax.rem(f // 2, 2), lax.rem(f, 2)


def neighbours():
    c, f, z, xh, y, xl, k = mesh_spot()
    z_up, z_down = lax.rem(z + 1, 4), lax.rem(z + 3, 4)
    y_up, y_down = lax.rem(y + 1, 4), lax.rem(y + 3, 4)
    side, far, twin = 4 * y + 2 * (1 - xl) + k, 2 * z + 1 - xh, 4 * y + 2 * xl + 1 - k
    return dict(
        far=(far, f),
        near=(c, side),
        back=(far, side),
        twin=(c, twin),
        z_up=(2 * z_up + xh, f),
        z_down=(2 * z_down + xh, f),
        y_up=(c, 4 * y_up + 2 * xl + k),
        y_down=(c, 4 * y_down + 2 * xl + k),
    )


def meet(peers):
    barrier = pltpu.get_barrier_semaphore()
    for peer in peers:
        pl.semaphore_signal(barrier, inc=1, device_id=peer, device_id_type=MESH)
    pl.semaphore_wait(barrier, len(peers))


class Flows:
    def __init__(self, send_sem, recv_sem):
        self.send_sem, self.recv_sem, self.made = send_sem, recv_sem, []

    def send(self, src, dst, peer):
        n = len(self.made)
        copy = pltpu.make_async_remote_copy(
            src_ref=src,
            dst_ref=dst,
            send_sem=self.send_sem.at[n],
            recv_sem=self.recv_sem.at[n],
            device_id=peer,
            device_id_type=MESH,
        )
        copy.start()
        self.made.append(copy)
        return copy

    def finish(self):
        for copy in self.made:
            copy.wait_send()


GATHER_FLOWS = 40


def gather_kernel(
    keys, values, grad, w, kv, w_all, datt, w_buf, total, send_sem, recv_sem, here_sem
):
    c, f, z, xh, y, xl, k = mesh_spot()
    at = neighbours()
    z_up, z_down, z_far = lax.rem(z + 1, 4), lax.rem(z + 3, 4), lax.rem(z + 2, 4)
    y_up, y_down, y_far = lax.rem(y + 1, 4), lax.rem(y + 3, 4), lax.rem(y + 2, 4)
    rows = keys.shape[0]
    half = w.shape[0] // 2
    meet(list(at.values()))
    flows = Flows(send_sem, recv_sem)

    def chunk(a, who):
        return kv.at[a, pl.ds(pl.multiple_of(who * rows, rows), rows), :]

    def shard(yy, xx, kk):
        return 4 * yy + 2 * xx + kk

    def whole(who):
        return w_buf.at[who]

    def part(who, p):
        return w_buf.at[who, pl.ds(p * half, half), :]

    own = (keys, values)
    kv_far = [flows.send(own[a], chunk(a, c), at["far"]) for a in (0, 1)]
    kv_up = [flows.send(own[a], chunk(a, c), at["z_up"]) for a in (0, 1)]
    kv_down = [flows.send(own[a], chunk(a, c), at["z_down"]) for a in (1, 0)][::-1]
    w_up = flows.send(w, whole(f), at["y_up"])
    w_down = flows.send(w, whole(f), at["y_down"])
    w_side = [
        flows.send(w.at[pl.ds(p * half, half), :], part(f, p), at[("near", "back")[p]])
        for p in (0, 1)
    ]
    to_twin = [flows.send(w, whole(f), at["twin"])]
    here = [
        pltpu.make_async_copy(keys, chunk(0, c), here_sem.at[0]),
        pltpu.make_async_copy(values, chunk(1, c), here_sem.at[1]),
        pltpu.make_async_copy(w, whole(f), here_sem.at[2]),
    ]
    for copy in here:
        copy.start()

    kv_up[0].wait_recv()
    on_k = flows.send(chunk(0, 2 * z_down + xh), chunk(0, 2 * z_down + xh), at["z_up"])
    kv_down[1].wait_recv()
    on_v = flows.send(chunk(1, 2 * z_up + xh), chunk(1, 2 * z_up + xh), at["z_down"])
    w_up.wait_recv()
    got = shard(y_down, xl, k)
    on_w0 = flows.send(part(got, 0), part(got, 0), at["y_up"])
    to_twin.append(flows.send(whole(got), whole(got), at["twin"]))
    w_down.wait_recv()
    got = shard(y_up, xl, k)
    on_w1 = flows.send(part(got, 1), part(got, 1), at["y_down"])
    to_twin.append(flows.send(whole(got), whole(got), at["twin"]))

    other = 2 * z + 1 - xh
    side = shard(y, 1 - xl, k)
    pair_up, pair_down = [None, None], [None, None]
    for a in (0, 1):
        kv_far[a].wait_recv()
        pair_up[a] = flows.send(chunk(a, other), chunk(a, other), at["z_up"])
        pair_down[a] = flows.send(chunk(a, other), chunk(a, other), at["z_down"])
    side_up, side_down = [], []
    for p in (0, 1):
        w_side[p].wait_recv()
        side_up.append(flows.send(part(side, p), part(side, p), at["y_up"]))
        side_down.append(flows.send(part(side, p), part(side, p), at["y_down"]))
    to_twin.append(flows.send(whole(side), whole(side), at["twin"]))

    def multiply(yy, first):
        def columns(n, carry):
            lanes = pl.ds(pl.multiple_of(n * 512, 512), 512)
            out = None
            for s in range(4):
                who = 4 * yy + s
                g = grad[:, pl.ds(pl.multiple_of(who * HEAD_DIM, HEAD_DIM), HEAD_DIM)]
                term = dot(g, w_buf[who, lanes, :], 1, 1)
                out = term if out is None else out + term
            total[:, lanes] = out if first else total[:, lanes] + out
            return carry

        lax.fori_loop(0, total.shape[1] // 512, columns, 0)

    kv_up[1].wait_recv()
    kv_down[0].wait_recv()
    got = shard(y_down, 1 - xl, k)
    side_up[0].wait_recv()
    on_s0 = flows.send(part(got, 0), part(got, 0), at["y_up"])
    side_up[1].wait_recv()
    to_twin.append(flows.send(whole(got), whole(got), at["twin"]))
    got = shard(y_up, 1 - xl, k)
    side_down[0].wait_recv()
    side_down[1].wait_recv()
    on_s1 = flows.send(part(got, 1), part(got, 1), at["y_down"])
    to_twin.append(flows.send(whole(got), whole(got), at["twin"]))

    pair_up[0].wait_recv()
    got = 2 * z_down + 1 - xh
    pair_on_k = flows.send(chunk(0, got), chunk(0, got), at["z_up"])
    pair_down[1].wait_recv()
    got = 2 * z_up + 1 - xh
    pair_on_v = flows.send(chunk(1, got), chunk(1, got), at["z_down"])

    got = shard(y_far, xl, k)
    on_w0.wait_recv()
    to_twin.append(flows.send(part(got, 0), part(got, 0), at["twin"]))
    on_w1.wait_recv()
    to_twin.append(flows.send(part(got, 1), part(got, 1), at["twin"]))
    for copy in here:
        copy.wait()
    for n in (0, 3):
        to_twin[n].wait_recv()
    multiply(y, True)
    for n in (1, 4):
        to_twin[n].wait_recv()
    multiply(y_down, False)
    for n in (2, 5):
        to_twin[n].wait_recv()
    multiply(y_up, False)

    got = shard(y_far, 1 - xl, k)
    on_s0.wait_recv()
    to_twin.append(flows.send(part(got, 0), part(got, 0), at["twin"]))
    on_s1.wait_recv()
    to_twin.append(flows.send(part(got, 1), part(got, 1), at["twin"]))
    for n in (6, 7, 8, 9):
        to_twin[n].wait_recv()
    multiply(y_far, False)
    out = pltpu.make_async_copy(w_buf, w_all, here_sem.at[3])
    out.start()
    datt[...] = total[...].astype(BF16)
    on_k.wait_recv()
    on_v.wait_recv()
    pair_up[1].wait_recv()
    pair_down[0].wait_recv()
    pair_on_k.wait_recv()
    pair_on_v.wait_recv()
    flows.finish()
    out.wait()


def gather(keys, values, grad, w):
    rows, kv_cols = keys.shape
    feats, cols = w.shape
    n_ctx, n_fsdp = lax.axis_size("ctx"), lax.axis_size("fsdp")
    hbm = pl.BlockSpec(memory_space=pltpu.HBM)
    vmem = pl.BlockSpec(memory_space=pltpu.VMEM)
    return pl.pallas_call(
        gather_kernel,
        in_specs=[hbm, hbm, vmem, hbm],
        out_specs=[hbm, hbm, vmem],
        out_shape=[
            jax.ShapeDtypeStruct((2, n_ctx * rows, kv_cols), BF16),
            jax.ShapeDtypeStruct((n_fsdp, feats, cols), BF16),
            jax.ShapeDtypeStruct((rows, feats), BF16),
        ],
        scratch_shapes=[
            pltpu.VMEM((n_fsdp, feats, cols), BF16),
            pltpu.VMEM((rows, feats), F32),
            pltpu.SemaphoreType.DMA((GATHER_FLOWS,)),
            pltpu.SemaphoreType.DMA((GATHER_FLOWS,)),
            pltpu.SemaphoreType.DMA((4,)),
        ],
        compiler_params=pltpu.CompilerParams(
            collective_id=0, has_side_effects=True, vmem_limit_bytes=40 << 20
        ),
        cost_estimate=pl.CostEstimate(
            flops=2 * rows * feats * feats, bytes_accessed=24 << 20, transcendentals=0
        ),
        name="gather",
    )(keys, values, grad, w)


def local(queries, keys, values, resid, grad_out, w_out, block_list, block_count):
    grad_rows = grad_out[0]
    kv, w_all, datt = gather(keys[0], values[0], grad_rows, w_out)
    w_whole = w_all.transpose(1, 0, 2).reshape(w_out.shape[0], -1)
    att, dq, dk, dv = attention(queries[0], datt, kv, block_list, block_count)
    feature_share = lax.psum_scatter(
        lax.dot_general(
            grad_rows, att, (((0,), (0,)), ((), ())), preferred_element_type=F32
        ).astype(BF16),
        "fsdp",
        scatter_dimension=0,
        tiled=True,
    )
    dkv = lax.psum_scatter(
        jnp.concatenate([dk, dv], axis=0), "ctx", scatter_dimension=1, tiled=True
    )
    mixed = (resid[0].astype(F32) + jnp.dot(att, w_whole, preferred_element_type=F32)).astype(BF16)
    proj = lax.psum_scatter(feature_share, "ctx", scatter_dimension=1, tiled=True).astype(F32).T
    return mixed[None], dq[None], dkv[:1], dkv[1:], proj


def solution(mesh):
    rows = P("fsdp", "ctx", None)
    in_specs = (rows, rows, rows, rows, rows, P(None, "fsdp"), P("ctx", None), P("ctx"))
    out_specs = (rows, rows, rows, rows, P("ctx", "fsdp"))
    return jax.shard_map(local, mesh=mesh, in_specs=in_specs, out_specs=out_specs, check_vma=False)
```

time: 544 us -> 374 us (0.69)
  waiting for transfers between devices: 320 us -> 230 us
  Pallas kernels: 0 us -> 76.7 us
  local copies, waits for them, and re-layouts: 103 us -> 34.9 us
  matrix products: 55.3 us -> 12.3 us
  other arithmetic: 46.2 us -> 5.42 us
    all_gather x3 -> x0, waiting for transfers between devices: 105 us -> none  [the longest x1 54.5 us: local(): lax.all_gather(values, 'ctx', axis=1, tiled=True)]
    pallas_call x0 -> x2, Pallas kernels: none -> 76.7 us  [the longest x1 50.9 us: gather(): pl.pallas_call(gather_kernel, in_specs=[hbm, hbm, vmem, hbm], out_specs=[...]
    reduce_scatter x1, waiting for transfers between devices: 0.01 us -> 71.4 us  [local(): lax.psum_scatter(feature_share, 'ctx', scatter_dimension=1, tiled=True)]
    reduce_scatter x2 -> x1, waiting for transfers between devices: 122 us -> 66.1 us  [local(): lax.psum_scatter(jnp.concatenate([dk, dv], axis=0), 'ctx', scatter_dimens...]
    dot_general x17 -> x2, matrix products: 55.3 us -> 12.3 us  [the longest x1 6.72 us: local(): jnp.dot(att, w_whole, preferred_element_type=F32)]
    gather x8 -> x0, local copies, waits for them, and re-layouts: 24.5 us -> none  [the longest x2 6.26 us: forward_block(): key_sel = jnp.take(blocked_keys, listed_blocks, axis=0)]
    while x46 -> x0, local copies, waits for them, and re-layouts: 19.5 us -> none
    scatter-add x2 -> x0, other arithmetic: 18.8 us -> none  [the longest x1 9.42 us: local(): key_holder = jnp.zeros((block_total, BLOCK_SIZE, KEY_VALUE_HEADS * HEAD_D...]
  transfers between devices with their start and end apart: 7 -> 3, of which waited for: 5 -> 3; matrix products, arithmetic and copies ran while one was open for 34% -> 7% of each run, Pallas kernels for 0% -> 0%
where the time goes in v1:
time: 374 us; the launch traced here: 373 us
  waiting for transfers between devices  230 us (61%)
  Pallas kernels  76.7 us (21%)
  local copies, waits for them, and re-layouts  34.9 us (9%)
  between operations  13.8 us (4%)
  matrix products  12.3 us (3%)
  other arithmetic  5.42 us (1%)
    unnamed x4, waiting for transfers between devices  92.2 us
    reduce_scatter x1, waiting for transfers between devices, local(): lax.psum_scatter(feature_share, 'ctx', scatter_dimension=1, tiled=True)  71.4 us
    reduce_scatter x1, waiting for transfers between devices, local(): lax.psum_scatter(jnp.concatenate([dk, dv], axis=0), 'ctx', scatter_dimens...  66.1 us
    pallas_call x1, Pallas kernels, gather(): pl.pallas_call(gather_kernel, in_specs=[hbm, hbm, vmem, hbm], out_specs=[...  50.9 us
    pallas_call x1, Pallas kernels, attention(): pl.pallas_call(attention_kernel, grid_spec=pltpu.PrefetchScalarGridSpec(n...  25.9 us
    unnamed x22, local copies, waits for them, and re-layouts  20.6 us
    transpose x1, local copies, waits for them, and re-layouts, local(): w_whole = w_all.transpose(1, 0, 2).reshape(w_out.shape[0], -1)  12.5 us
  transfers between devices with their start and end apart: 3, of which 3 were waited for; matrix products, arithmetic and copies ran while one was open for 7% of the time, Pallas kernels for 0%

profile of v1, /device:TPU:0, one launch (start us, length us, event | category | flops | bytes accessed | tf_op | source)
XLA Modules:
  0.0 373.0 jit_solution(7639712037354733712)
XLA Ops:
  7.2 0.0 reduce-scatter.10.cloned.1.call-start
  7.2 1.2 copy-done
  8.5 1.0 copy-done.3
  9.5 0.9 copy-done.4
  10.5 0.9 copy-done.5
  11.4 50.9 %gather.1 = (bf16[2,2048,512]{2,1,0:T(8,128)(2,1)S(1)}, bf16[16,2048,128]{2,1,0:T(8,128)(2,1)}, bf16[256,2048]{1,0:T(8,128)(2,1)S(1)}) custom-call(bf16[256,512]{1,0:T(8,128)(2,1)S(1)} %bitcast.24, bf16[256,512]{1,0:T(8,128)(2,1)S(1)} %bitcast.25, bf16[256,2048]{1,0:T(8,128)(2,1)S(1)} %bitcast.22, bf16[2048,128]{1,0:T(8,128)(2,1)S(1)} %copy-done.3), custom_call_target="tpu_custom_call" | custom-call | flops 2147483648 | bytes 25165824 | tf_op jit(solution)/shard_map/gather/pallas_call | solution.py:323
  62.3 2.0 copy-done.8
  64.3 25.9 %attention.1 = (bf16[256,2048]{1,0:T(8,128)(2,1)S(1)}, bf16[256,2048]{1,0:T(8,128)(2,1)}, bf16[1,2048,512]{2,1,0:T(8,128)(2,1)S(1)}, bf16[1,2048,512]{2,1,0:T(8,128)(2,1)}) custom-call(s32[2,8]{1,0:T(2,128)S(1)} %copy-done.6, s32[2]{0:T(128)S(1)} %copy-done.7, bf16[256,2048]{1,0:T(8,128)(2,1)S(1)} %bitcast.23, ...), custom_call_target="tpu_custom_call" | custom-call | flops 6442450944 | bytes 12582912 | tf_op jit(solution)/shard_map/attention/pallas_call | solution.py:95
  90.2 5.6 %convert_bitcast_fusion = bf16[2048,2048]{0,1:T(8,128)(2,1)} fusion(bf16[256,2048]{1,0:T(8,128)(2,1)S(1)} %get-tuple-element.14, bf16[1,256,2048]{2,1,0:T(8,128)(2,1)S(1)} %copy-done.1), kind=kOutput, calls=%fused_computation | convolution fusion | flops 2151677952 | bytes 10485760 | tf_op jit(solution)/shard_map/dot_general | solution.py:355
  95.8 12.4 %copy.15 = bf16[2048,2048]{1,0:T(8,128)(2,1)} copy(bf16[2048,2048]{0,1:T(8,128)(2,1)} %convert_bitcast_fusion) | data formatting | bytes 16777216
  108.1 0.0 reduce-scatter.10.cloned.1.call-update
  108.2 0.0 reduce-scatter.6.cloned.1.call-start
  108.2 3.9 %pad_maximum_fusion = bf16[2,2048,512]{2,1,0:T(8,128)(2,1)} fusion(bf16[1,2048,512]{2,1,0:T(8,128)(2,1)} %get-tuple-element.18, bf16[1,2048,512]{2,1,0:T(8,128)(2,1)S(1)} %get-tuple-element.17), kind=kLoop, calls=%fused_computation.1 | loop fusion | flops 2097152 | bytes 8388608 | tf_op jit(solution)/shard_map/concatenate | solution.py:363
  112.1 0.0 reduce-scatter.6.cloned.1.call-update
  112.1 0.0 reduce-scatter.8.cloned.1.call-start
  112.2 92.2 %reduce-scatter.10.cloned.1.call-done = bf16[128,2048]{1,0:T(8,128)(2,1)} async-done(((bf16[2048,2048]{1,0:T(8,128)(2,1)}), bf16[128,2048]{1,0:T(8,128)(2,1)}) %reduce-scatter.10.cloned.1.call-update) | async-done | bytes 524304
  204.4 2.0 copy.16
  206.4 0.0 reduce-scatter.8.cloned.1.call-update
  206.5 12.5 %copy.14 = bf16[2048,16,128]{0,2,1:T(8,128)(2,1)} copy(bf16[2048,16,128]{2,0,1:T(8,128)(2,1)} %bitcast.26) | data formatting | bytes 16777216 | tf_op jit(solution)/shard_map/transpose | solution.py:352
  218.9 6.7 %fusion.1 = bf16[1,256,2048]{2,1,0:T(8,128)(2,1)} fusion(bf16[256,2048]{1,0:T(8,128)(2,1)S(1)} %get-tuple-element.14, bf16[2048,2048]{0,1:T(8,128)(2,1)} %bitcast.27, bf16[1,256,2048]{2,1,0:T(8,128)(2,1)S(1)} %copy-done.9), kind=kOutput, calls=%fused_computation.4 | convolution fusion | flops 2149056512 | bytes 11534336 | tf_op jit(solution)/shard_map/dot_general | solution.py:365
  225.7 66.1 %reduce-scatter.6.cloned.1.call-done = bf16[2,256,512]{2,1,0:T(8,128)(2,1)} async-done(((bf16[2,2048,512]{2,1,0:T(8,128)(2,1)}), bf16[2,256,512]{2,1,0:T(8,128)(2,1)}) %reduce-scatter.6.cloned.1.call-update) | async-done | bytes 524304 | tf_op jit(solution)/shard_map/reduce_scatter | solution.py:362
  291.7 1.9 fusion.3
  293.6 71.4 %reduce-scatter.8.cloned.1.call-done = bf16[128,256]{0,1:T(8,128)(2,1)} async-done(((bf16[128,2048]{0,1:T(8,128)(2,1)}), bf16[128,256]{0,1:T(8,128)(2,1)}) %reduce-scatter.8.cloned.1.call-update) | async-done | bytes 65552 | tf_op jit(solution)/shard_map/reduce_scatter | solution.py:366
  365.0 1.5 convert_bitcast_fusion.1
  (15 shorter events, 0.0 us)
Async XLA Ops:
  7.2 57.1 %copy-start.6 = (s32[2,8]{1,0:T(2,128)S(1)}, s32[2,8]{1,0:T(2,128)}, u32[]{:S(2)}) copy-start(s32[2,8]{1,0:T(2,128)} %list_ref.1) | copy-start | bytes 196
  7.2 57.1 %copy-start.7 = (s32[2]{0:T(128)S(1)}, s32[2]{0:T(128)}, u32[]{:S(2)}) copy-start(s32[2]{0:T(128)} %count_ref.1) | copy-start | bytes 28
  7.2 197.2 %reduce-scatter.10.cloned.1.call-start = ((), (), s32[]{:S(2)}) async-start(), calls=%async_computation.5 | async-start | bytes 8912896
  7.2 1.2 copy-start
  8.5 1.0 copy-start.3
  9.5 0.9 copy-start.4
  10.5 0.9 copy-start.5
  11.4 52.9 %copy-start.2 = (bf16[1,256,2048]{2,1,0:T(8,128)(2,1)S(1)}, bf16[1,256,2048]{2,1,0:T(8,128)(2,1)}, u32[]{:S(2)}) copy-start(bf16[1,256,2048]{2,1,0:T(8,128)(2,1)} %param.8) | copy-start | bytes 3145732
  62.3 2.0 copy-start.8
  64.3 25.9 %copy-start.1 = (bf16[1,256,2048]{2,1,0:T(8,128)(2,1)S(1)}, bf16[1,256,2048]{2,1,0:T(8,128)(2,1)}, u32[]{:S(2)}) copy-start(bf16[1,256,2048]{2,1,0:T(8,128)(2,1)} %param.12) | copy-start | bytes 3145732
  108.2 183.6 %reduce-scatter.6.cloned.1.call-start = ((), (), s32[]{:S(2)}) async-start(), calls=%async_computation.3 | async-start | bytes 4718592 | tf_op jit(solution)/shard_map/reduce_scatter | solution.py:362
  112.1 252.8 %reduce-scatter.8.cloned.1.call-start = ((), (), s32[]{:S(2)}) async-start(), calls=%async_computation.4 | async-start | bytes 589824 | tf_op jit(solution)/shard_map/reduce_scatter | solution.py:366
  206.4 12.5 %copy-start.9 = (bf16[1,256,2048]{2,1,0:T(8,128)(2,1)S(1)}, bf16[1,256,2048]{2,1,0:T(8,128)(2,1)}, u32[]{:S(2)}) copy-start(bf16[1,256,2048]{2,1,0:T(8,128)(2,1)} %param.11) | copy-start | bytes 3145732
Sparse Core Ops, SparseCore 0:
  108.3 96.0 reduce-scatter.9
  208.2 83.4 reduce-scatter.5
  295.7 69.2 reduce-scatter.7

commit v2 on v1

--- a/solution.py
+++ b/solution.py
@@ -30,7 +30,7 @@
 
 
 def attention_kernel(
-    list_ref, count_ref, q_ref, do_ref, k_ref, v_ref, att_ref, dq_ref, dk_ref, dv_ref, dk_acc, dv_acc
+    list_ref, count_ref, q_ref, do_ref, k_ref, v_ref, att_ref, att_t_ref, dq_ref, dk_ref, dv_ref, dk_acc, dv_acc
 ):
     i = pl.program_id(1)
     cols = GROUP * BLOCK
@@ -69,6 +69,7 @@
     dv_sel = dot(pb, do4, 1, 0)
     for h in range(GROUP):
         att_ref[:, h * HEAD_DIM : (h + 1) * HEAD_DIM] = o4[h * BLOCK : (h + 1) * BLOCK]
+        att_t_ref[h] = o_t[:, h * BLOCK : (h + 1) * BLOCK].astype(BF16)
         dq_ref[:, h * HEAD_DIM : (h + 1) * HEAD_DIM] = dq4[h * BLOCK : (h + 1) * BLOCK]
     for j in range(SLOTS):
         dk_acc[rows[j], :] += dk_sel[j * BLOCK : (j + 1) * BLOCK]
@@ -76,8 +77,8 @@
 
     @pl.when(i == pl.num_programs(1) - 1)
     def _():
-        dk_ref[0] = dk_acc[...].astype(BF16)
-        dv_ref[0] = dv_acc[...].astype(BF16)
+        dk_ref[...] = dk_acc[...].astype(BF16)
+        dv_ref[...] = dv_acc[...].astype(BF16)
 
 
 def attention(queries, datt, kv, block_list, block_count):
@@ -90,7 +91,8 @@
     def kv_spec(which):
         return pl.BlockSpec((1, seq, HEAD_DIM), lambda g, i, *_: (which, 0, g))
 
-    out_spec = pl.BlockSpec((1, seq, HEAD_DIM), lambda g, i, *_: (0, 0, g))
+    out_spec = pl.BlockSpec((seq, HEAD_DIM), lambda g, i, *_: (0, g))
+    t_spec = pl.BlockSpec((GROUP, HEAD_DIM, BLOCK), lambda g, i, *_: (g, 0, i))
     flops = 12 * rows * QUERY_HEADS * SLOTS * BLOCK * HEAD_DIM
     return pl.pallas_call(
         attention_kernel,
@@ -98,14 +100,15 @@
             num_scalar_prefetch=2,
             grid=(KV_HEADS, rows // BLOCK),
             in_specs=[q_spec, q_spec, kv_spec(0), kv_spec(1)],
-            out_specs=[q_spec, q_spec, out_spec, out_spec],
+            out_specs=[q_spec, t_spec, q_spec, out_spec, out_spec],
             scratch_shapes=[pltpu.VMEM((seq, HEAD_DIM), F32)] * 2,
         ),
         out_shape=[
             jax.ShapeDtypeStruct((rows, width), BF16),
+            jax.ShapeDtypeStruct((QUERY_HEADS, HEAD_DIM, rows), BF16),
             jax.ShapeDtypeStruct((rows, width), BF16),
-            jax.ShapeDtypeStruct((1, seq, kv_cols), BF16),
-            jax.ShapeDtypeStruct((1, seq, kv_cols), BF16),
+            jax.ShapeDtypeStruct((seq, kv_cols), BF16),
+            jax.ShapeDtypeStruct((seq, kv_cols), BF16),
         ],
         compiler_params=pltpu.CompilerParams(
             dimension_semantics=("arbitrary", "arbitrary"), vmem_limit_bytes=48 << 20
@@ -173,7 +176,7 @@
 
 
 def gather_kernel(
-    keys, values, grad, w, kv, w_all, datt, w_buf, total, send_sem, recv_sem, here_sem
+    keys, values, grad, w, kv, w_all, datt, grad_twin, w_buf, total, send_sem, recv_sem, here_sem
 ):
     c, f, z, xh, y, xl, k = mesh_spot()
     at = neighbours()
@@ -207,6 +210,7 @@
         for p in (0, 1)
     ]
     to_twin = [flows.send(w, whole(f), at["twin"])]
+    swap = flows.send(grad, grad_twin, at["twin"])
     here = [
         pltpu.make_async_copy(keys, chunk(0, c), here_sem.at[0]),
         pltpu.make_async_copy(values, chunk(1, c), here_sem.at[1]),
@@ -304,6 +308,7 @@
     out = pltpu.make_async_copy(w_buf, w_all, here_sem.at[3])
     out.start()
     datt[...] = total[...].astype(BF16)
+    swap.wait_recv()
     on_k.wait_recv()
     on_v.wait_recv()
     pair_up[1].wait_recv()
@@ -323,11 +328,12 @@
     return pl.pallas_call(
         gather_kernel,
         in_specs=[hbm, hbm, vmem, hbm],
-        out_specs=[hbm, hbm, vmem],
+        out_specs=[hbm, hbm, vmem, hbm],
         out_shape=[
             jax.ShapeDtypeStruct((2, n_ctx * rows, kv_cols), BF16),
             jax.ShapeDtypeStruct((n_fsdp, feats, cols), BF16),
             jax.ShapeDtypeStruct((rows, feats), BF16),
+            jax.ShapeDtypeStruct(grad.shape, BF16),
         ],
         scratch_shapes=[
             pltpu.VMEM((n_fsdp, feats, cols), BF16),
@@ -346,25 +352,286 @@
     )(keys, values, grad, w)
 
 
+REDUCE_FLOWS = 41
+PIECES = 2
+
+
+def reduce_kernel(
+    dk, dv, att, att_t, grad, grad_twin, resid, w_all,
+    mixed, dk_out, dv_out, proj,
+    att_twin, w_buf, att_buf, res_buf, ahead, mine, hop_in, raw_in, sum_in, sum_out, kept, far_out, far_in,
+    far_p, up_keep, down_keep, own_keep, up_raw, down_raw, top_in, low_in, top_out, low_out,
+    top_raw, low_raw, top_sum, low_sum, x_out, x_in, x_keep, z_out, z_in, z_keep,
+    send_sem, recv_sem, here_sem,
+):
+    c, f, z, xh, y, xl, k = mesh_spot()
+    at = neighbours()
+    z_up, z_down, z_far = lax.rem(z + 1, 4), lax.rem(z + 3, 4), lax.rem(z + 2, 4)
+    y_up, y_down, y_far = lax.rem(y + 1, 4), lax.rem(y + 3, 4), lax.rem(y + 2, 4)
+    at["z_far"] = (2 * z_far + xh, f)
+    rows, kv_cols = dk_out.shape
+    pair = 2 * rows
+    wide = kv_cols // PIECES
+    meet(list(at.values()))
+    flows = Flows(send_sem, recv_sem)
+    parts = (dk, dv)
+
+    def block(a, zz, p):
+        return parts[a].at[
+            pl.ds(pl.multiple_of(zz * pair, pair), pair), pl.ds(p * wide, wide)
+        ]
+
+    swap = flows.send(att_t, att_twin, at["twin"])
+    hops = [
+        [
+            flows.send(block(0, z_far, p), hop_in.at[0, p], at["z_up"]),
+            flows.send(block(1, z_far, p), hop_in.at[1, p], at["z_down"]),
+        ]
+        for p in range(PIECES)
+    ]
+    here = []
+    for n, (src, dst) in enumerate(
+        [
+            (dk.at[pl.ds(pl.multiple_of(z_up * pair, pair), pair), :], ahead.at[0]),
+            (dv.at[pl.ds(pl.multiple_of(z_down * pair, pair), pair), :], ahead.at[1]),
+            (dk.at[pl.ds(pl.multiple_of(z * pair, pair), pair), :], mine.at[0]),
+            (dv.at[pl.ds(pl.multiple_of(z * pair, pair), pair), :], mine.at[1]),
+            (w_all, w_buf),
+            (att, att_buf),
+            (resid, res_buf),
+        ]
+    ):
+        copy = pltpu.make_async_copy(src, dst, here_sem.at[n])
+        copy.start()
+        here.append(copy)
+
+    def product(yy, p, low, store):
+        lanes = [
+            pl.ds(pl.multiple_of((4 * yy + 2 * s + k) * HEAD_DIM, HEAD_DIM), HEAD_DIM)
+            for s in (0, 1)
+        ]
+        g_own = jnp.concatenate([grad[:, s] for s in lanes], axis=1)
+        g_twin = jnp.concatenate([grad_twin[:, s] for s in lanes], axis=1)
+
+        def one(m, carry):
+            head = 2 * (m + low) + p
+            store(m, dot(att_t[head], g_own, 1, 0) + dot(att_twin[head], g_twin, 1, 0))
+            return carry
+
+        lax.fori_loop(0, 4, one, 0)
+
+    def put(ref, p, low=0):
+        def store(m, value):
+            ref[p, m + low] = value.astype(ref.dtype)
+
+        return store
+
+    swap.wait_recv()
+    top_hop, low_hop = [], []
+    for p in range(PIECES):
+        product(y_far, p, 0, put(far_p, p))
+        top_hop.append(flows.send(far_p.at[p, pl.ds(0, 4)], top_in.at[p], at["y_up"]))
+        product(y_far, p, 4, put(far_p, p, 4))
+        low_hop.append(flows.send(far_p.at[p, pl.ds(4, 4)], low_in.at[p], at["y_down"]))
+    raws = [
+        [
+            flows.send(block(0, z_down, p), raw_in.at[0, p], at["z_down"]),
+            flows.send(block(1, z_up, p), raw_in.at[1, p], at["z_up"]),
+        ]
+        for p in range(PIECES)
+    ]
+    raw_top, raw_low = [], []
+    for p in range(PIECES):
+        product(y_up, p, 4, put(up_raw, p))
+        raw_low.append(flows.send(up_raw.at[p], low_raw.at[p], at["y_up"]))
+        product(y_down, p, 0, put(down_raw, p))
+        raw_top.append(flows.send(down_raw.at[p], top_raw.at[p], at["y_down"]))
+        product(y_up, p, 0, put(up_keep, p))
+        product(y_down, p, 4, put(down_keep, p))
+
+    for copy in here[:4]:
+        copy.wait()
+    sums = [[None, None] for _ in range(PIECES)]
+    top_on, low_on = [], []
+    for p in range(PIECES):
+        cols = slice(p * wide, (p + 1) * wide)
+        for a, towards in ((0, "z_up"), (1, "z_down")):
+            hops[p][a].wait_recv()
+            sum_out[a, p] = (ahead[a, :, cols].astype(F32) + hop_in[a, p].astype(F32)).astype(BF16)
+            sums[p][a] = flows.send(sum_out.at[a, p], sum_in.at[a, p], at[towards])
+        top_hop[p].wait_recv()
+        top_out[p] = (up_keep[p] + top_in[p].astype(F32)).astype(BF16)
+        top_on.append(flows.send(top_out.at[p], top_sum.at[p], at["y_up"]))
+        low_hop[p].wait_recv()
+        low_out[p] = (down_keep[p] + low_in[p].astype(F32)).astype(BF16)
+        low_on.append(flows.send(low_out.at[p], low_sum.at[p], at["y_down"]))
+    for p in range(PIECES):
+        product(y, p, 0, put(own_keep, p))
+        product(y, p, 4, put(own_keep, p, 4))
+
+    for copy in here[4:]:
+        copy.wait()
+
+    def project(n, carry):
+        lanes = pl.ds(pl.multiple_of(n * HEAD_DIM, HEAD_DIM), HEAD_DIM)
+        out = dot(att_buf[...], w_buf[n], 1, 0)
+        mixed[:, lanes] = (res_buf[:, lanes].astype(F32) + out).astype(BF16)
+        return carry
+
+    lax.fori_loop(0, w_buf.shape[0], project, 0)
+
+    keep_rows = pl.ds(pl.multiple_of(xh * rows, rows), rows)
+    give_rows = pl.ds(pl.multiple_of((1 - xh) * rows, rows), rows)
+    fars = [[None, None] for _ in range(PIECES)]
+    x_to = ("near", "far", "back")
+    x_flow = []
+    for p in range(PIECES):
+        cols = pl.ds(p * wide, wide)
+        for a in (0, 1):
+            raws[p][a].wait_recv()
+            sums[p][a].wait_recv()
+
+            def gathered(which):
+                return (
+                    mine[a, which, cols].astype(F32)
+                    + raw_in[a, p, which, :].astype(F32)
+                    + sum_in[a, p, which, :].astype(F32)
+                )
+
+            far_out[a, p] = gathered(give_rows).astype(BF16)
+            fars[p][a] = flows.send(far_out.at[a, p], far_in.at[a, p], at["far"])
+            kept[a, p] = gathered(keep_rows)
+
+        raw_top[p].wait_recv()
+        top_on[p].wait_recv()
+        raw_low[p].wait_recv()
+        low_on[p].wait_recv()
+        for m in range(4):
+            own_keep[p, m] += top_raw[p, m].astype(F32) + top_sum[p, m].astype(F32)
+            own_keep[p, m + 4] += low_raw[p, m].astype(F32) + low_sum[p, m].astype(F32)
+        near_lanes = pl.ds(pl.multiple_of((1 - xl) * HEAD_DIM, HEAD_DIM), HEAD_DIM)
+        own_lanes = pl.ds(pl.multiple_of(xl * HEAD_DIM, HEAD_DIM), HEAD_DIM)
+        sent = []
+        for n, (hi, lanes) in enumerate(
+            ((xh, near_lanes), (1 - xh, own_lanes), (1 - xh, near_lanes))
+        ):
+            for zz in range(4):
+                x_out[p, n, zz] = own_keep[p, 2 * zz + hi, :, lanes].astype(BF16)
+            sent.append(flows.send(x_out.at[p, n], x_in.at[p, n], at[x_to[n]]))
+        x_flow.append(sent)
+        for zz in range(4):
+            x_keep[p, zz] = own_keep[p, 2 * zz + xh, :, own_lanes]
+
+    z_to = (("z_up", z_up), ("z_down", z_down), ("z_far", z_far))
+    z_flow = []
+    for p in range(PIECES):
+        cols = slice(p * wide, (p + 1) * wide)
+        for a, out in ((0, dk_out), (1, dv_out)):
+            fars[p][a].wait_recv()
+            out[:, cols] = (kept[a, p] + far_in[a, p].astype(F32)).astype(BF16)
+        for n in range(3):
+            x_flow[p][n].wait_recv()
+        for zz in range(4):
+            total = x_keep[p, zz]
+            for n in range(3):
+                total += x_in[p, n, zz].astype(F32)
+            x_keep[p, zz] = total
+        sent = []
+        for n, (name, zz) in enumerate(z_to):
+            z_out[p, n] = x_keep[p, zz].astype(BF16)
+            sent.append(flows.send(z_out.at[p, n], z_in.at[p, n], at[name]))
+        z_flow.append(sent)
+        z_keep[p] = x_keep[p, z]
+    for p in range(PIECES):
+        total = z_keep[p]
+        for n in range(3):
+            z_flow[p][n].wait_recv()
+            total += z_in[p, n].astype(F32)
+        proj[pl.ds(p * HEAD_DIM, HEAD_DIM), :] = total
+    flows.finish()
+
+
+def reduce(dk, dv, att, att_t, grad, grad_twin, resid, w_all):
+    n_ctx = lax.axis_size("ctx")
+    seq, kv_cols = dk.shape
+    rows, feats = att.shape
+    chunk = seq // n_ctx
+    heads = att_t.shape[0]
+    per = heads // n_ctx
+    wide = kv_cols // PIECES
+    hbm = pl.BlockSpec(memory_space=pltpu.HBM)
+    vmem = pl.BlockSpec(memory_space=pltpu.VMEM)
+
+    def quad(dtype, n=4, lanes=2 * HEAD_DIM):
+        return pltpu.VMEM((PIECES, n, HEAD_DIM, lanes), dtype)
+
+    def kv_buf(height, dtype=BF16):
+        return pltpu.VMEM((2, PIECES, height, wide), dtype)
+
+    return pl.pallas_call(
+        reduce_kernel,
+        in_specs=[hbm, hbm, hbm, vmem, vmem, vmem, hbm, hbm],
+        out_specs=[vmem] * 4,
+        out_shape=[
+            jax.ShapeDtypeStruct((rows, feats), BF16),
+            jax.ShapeDtypeStruct((chunk, kv_cols), BF16),
+            jax.ShapeDtypeStruct((chunk, kv_cols), BF16),
+            jax.ShapeDtypeStruct((per * HEAD_DIM, HEAD_DIM), F32),
+        ],
+        scratch_shapes=[
+            pltpu.VMEM(att_t.shape, BF16),
+            pltpu.VMEM(w_all.shape, BF16),
+            pltpu.VMEM(att.shape, BF16),
+            pltpu.VMEM(resid.shape, BF16),
+            pltpu.VMEM((2, 2 * chunk, kv_cols), BF16),
+            pltpu.VMEM((2, 2 * chunk, kv_cols), BF16),
+            kv_buf(2 * chunk),
+            kv_buf(2 * chunk),
+            kv_buf(2 * chunk),
+            kv_buf(2 * chunk),
+            kv_buf(chunk, F32),
+            kv_buf(chunk),
+            kv_buf(chunk),
+            quad(BF16, 8),
+            quad(F32),
+            quad(F32),
+            quad(F32, 8),
+            quad(BF16),
+            quad(BF16),
+            quad(BF16),
+            quad(BF16),
+            quad(BF16),
+            quad(BF16),
+            quad(BF16),
+            quad(BF16),
+            quad(BF16),
+            quad(BF16),
+            pltpu.VMEM((PIECES, 3, 4, HEAD_DIM, HEAD_DIM), BF16),
+            pltpu.VMEM((PIECES, 3, 4, HEAD_DIM, HEAD_DIM), BF16),
+            quad(F32, 4, HEAD_DIM),
+            quad(BF16, 3, HEAD_DIM),
+            quad(BF16, 3, HEAD_DIM),
+            pltpu.VMEM((PIECES, HEAD_DIM, HEAD_DIM), F32),
+            pltpu.SemaphoreType.DMA((REDUCE_FLOWS,)),
+            pltpu.SemaphoreType.DMA((REDUCE_FLOWS,)),
+            pltpu.SemaphoreType.DMA((7,)),
+        ],
+        compiler_params=pltpu.CompilerParams(
+            collective_id=1, has_side_effects=True, vmem_limit_bytes=52 << 20
+        ),
+        cost_estimate=pl.CostEstimate(
+            flops=4 * rows * feats * feats, bytes_accessed=24 << 20, transcendentals=0
+        ),
+        name="reduce",
+    )(dk, dv, att, att_t, grad, grad_twin, resid, w_all)
+
+
 def local(queries, keys, values, resid, grad_out, w_out, block_list, block_count):
-    grad_rows = grad_out[0]
-    kv, w_all, datt = gather(keys[0], values[0], grad_rows, w_out)
-    w_whole = w_all.transpose(1, 0, 2).reshape(w_out.shape[0], -1)
-    att, dq, dk, dv = attention(queries[0], datt, kv, block_list, block_count)
-    feature_share = lax.psum_scatter(
-        lax.dot_general(
-            grad_rows, att, (((0,), (0,)), ((), ())), preferred_element_type=F32
-        ).astype(BF16),
-        "fsdp",
-        scatter_dimension=0,
-        tiled=True,
-    )
-    dkv = lax.psum_scatter(
-        jnp.concatenate([dk, dv], axis=0), "ctx", scatter_dimension=1, tiled=True
-    )
-    mixed = (resid[0].astype(F32) + jnp.dot(att, w_whole, preferred_element_type=F32)).astype(BF16)
-    proj = lax.psum_scatter(feature_share, "ctx", scatter_dimension=1, tiled=True).astype(F32).T
-    return mixed[None], dq[None], dkv[:1], dkv[1:], proj
+    grad = grad_out[0]
+    kv, w_all, datt, grad_twin = gather(keys[0], values[0], grad, w_out)
+    att, att_t, dq, dk, dv = attention(queries[0], datt, kv, block_list, block_count)
+    mixed, dk, dv, proj = reduce(dk, dv, att, att_t, grad, grad_twin, resid[0], w_all)
+    return mixed[None], dq[None], dk[None], dv[None], proj
 
 
 def solution(mesh):

time: 374 us -> 154 us (0.41)
  waiting for transfers between devices: 230 us -> 0 us
  Pallas kernels: 76.7 us -> 141 us
  local copies, waits for them, and re-layouts: 34.9 us -> 12.2 us
  between operations: 13.8 us -> 0.69 us
  matrix products: 12.3 us -> 0 us
  other arithmetic: 5.42 us -> 0 us
    reduce_scatter x2 -> x0, waiting for transfers between devices: 137 us -> none  [the longest x1 71.4 us: local(): lax.psum_scatter(feature_share, 'ctx', scatter_dimension=1, tiled=True)]
    unnamed x4 -> x0, waiting for transfers between devices: 92.2 us -> none
    pallas_call x0 -> x1, Pallas kernels: none -> 64.2 us  [reduce(): pl.pallas_call(reduce_kernel, in_specs=[hbm, hbm, hbm, vmem, vmem, vmem,...]
    transpose x1 -> x0, local copies, waits for them, and re-layouts: 12.5 us -> none  [local(): w_whole = w_all.transpose(1, 0, 2).reshape(w_out.shape[0], -1)]
    dot_general x2 -> x0, matrix products: 12.3 us -> none  [the longest x1 6.72 us: local(): jnp.dot(att, w_whole, preferred_element_type=F32)]
    unnamed x22 -> x26, local copies, waits for them, and re-layouts: 20.6 us -> 12.2 us
    concatenate x1 -> x0, other arithmetic: 3.91 us -> none  [local(): jnp.concatenate([dk, dv], axis=0)]
  transfers between devices with their start and end apart: 3 -> 0, of which waited for: 3 -> 0; matrix products, arithmetic and copies ran while one was open for 7% -> 0% of each run, Pallas kernels for 0% -> 0%
where the time goes in v2:
time: 154 us
  Pallas kernels  141 us (92%)
  local copies, waits for them, and re-layouts  12.2 us (8%)
    pallas_call x1, Pallas kernels, reduce(): pl.pallas_call(reduce_kernel, in_specs=[hbm, hbm, hbm, vmem, vmem, vmem,...  64.2 us
    pallas_call x1, Pallas kernels, gather(): pl.pallas_call(gather_kernel, in_specs=[hbm, hbm, vmem, hbm], out_specs=[...  50.9 us
    pallas_call x1, Pallas kernels, attention(): pl.pallas_call(attention_kernel, grid_spec=pltpu.PrefetchScalarGridSpec(n...  25.9 us
    unnamed x26, local copies, waits for them, and re-layouts  12.2 us

profile of v2, /device:TPU:0, one launch (start us, length us, event | category | flops | bytes accessed | tf_op | source)
XLA Modules:
  0.0 153.9 jit_solution(14159051453995325009)
XLA Ops:
  0.6 0.0 copy-start.9
  0.6 0.0 copy-start.8
  0.7 0.0 copy-start
  0.7 1.2 copy-done
  1.9 0.0 copy-start.5
  1.9 1.0 copy-done.5
  2.9 0.0 copy-start.6
  2.9 0.9 copy-done.6
  3.9 0.9 copy-done.7
  4.8 50.9 %gather.1 = (bf16[2,2048,512]{2,1,0:T(8,128)(2,1)S(1)}, bf16[16,2048,128]{2,1,0:T(8,128)(2,1)}, bf16[256,2048]{1,0:T(8,128)(2,1)S(1)}, bf16[256,2048]{1,0:T(8,128)(2,1)S(1)}) custom-call(bf16[256,512]{1,0:T(8,128)(2,1)S(1)} %bitcast.15, bf16[256,512]{1,0:T(8,128)(2,1)S(1)} %bitcast.16, bf16[256,2048]{1,0:T(8,128)(2,1)S(1)} %bitcast.10, ...), custom_call_target="tpu_custom_call" | custom-call | flops 2147483648 | bytes 25165824 | tf_op jit(solution)/shard_map/gather/pallas_call | solution.py:328
  55.7 0.0 copy-start.1
  55.7 1.0 copy-done.1
  56.7 2.0 %copy-done.10 = bf16[2,2048,512]{2,1,0:T(8,128)(2,1)} copy-done((bf16[2,2048,512]{2,1,0:T(8,128)(2,1)}, bf16[2,2048,512]{2,1,0:T(8,128)(2,1)S(1)}, u32[]{:S(2)}) %copy-start.10) | copy-done | bytes 4194328
  58.7 0.0 copy-done.9
  58.7 0.0 copy-done.8
  58.7 0.0 copy-done.4
  58.7 25.9 %attention.1 = (bf16[256,2048]{1,0:T(8,128)(2,1)S(1)}, bf16[16,128,256]{2,1,0:T(8,128)(2,1)S(1)}, bf16[256,2048]{1,0:T(8,128)(2,1)}, bf16[2048,512]{1,0:T(8,128)(2,1)}, bf16[2048,512]{1,0:T(8,128)(2,1)}) custom-call(s32[2,8]{1,0:T(2,128)S(1)} %copy-done.8, s32[2]{0:T(128)S(1)} %copy-done.9, bf16[256,2048]{1,0:T(8,128)(2,1)S(1)} %bitcast.14, ...), custom_call_target="tpu_custom_call" | custom-call | flops 6442450944 | bytes 12582912 | tf_op jit(solution)/shard_map/attention/pallas_call | solution.py:97
  84.6 1.0 copy-done.2
  85.6 1.1 copy-done.3
  86.7 64.2 %reduce.1 = (bf16[256,2048]{1,0:T(8,128)(2,1)S(1)}, bf16[256,512]{1,0:T(8,128)(2,1)S(1)}, bf16[256,512]{1,0:T(8,128)(2,1)S(1)}, f32[256,128]{1,0:T(8,128)S(1)}) custom-call(bf16[2048,512]{1,0:T(8,128)(2,1)} %get-tuple-element.20.dk, bf16[2048,512]{1,0:T(8,128)(2,1)} %get-tuple-element.21.dv, bf16[256,2048]{1,0:T(8,128)(2,1)} %copy-done.2, ...), custom_call_target="tpu_custom_call" | custom-call | flops 4294967296 | bytes 25165824 | tf_op jit(solution)/shard_map/reduce/pallas_call | solution.py:571
  150.9 1.0 copy.17
  151.9 0.7 copy.18
  152.6 0.7 copy.19
  153.3 0.7 copy.20
  (5 shorter events, 0.0 us)
Async XLA Ops:
  0.6 58.0 %copy-start.9 = (s32[2]{0:T(128)S(1)}, s32[2]{0:T(128)}, u32[]{:S(2)}) copy-start(s32[2]{0:T(128)} %count_ref.1) | copy-start | bytes 28
  0.6 58.0 %copy-start.8 = (s32[2,8]{1,0:T(2,128)S(1)}, s32[2,8]{1,0:T(2,128)}, u32[]{:S(2)}) copy-start(s32[2,8]{1,0:T(2,128)} %list_ref.1) | copy-start | bytes 196
  0.7 1.2 copy-start
  1.9 1.0 copy-start.5
  2.9 0.9 copy-start.6
  3.9 0.9 copy-start.7
  4.8 53.8 %copy-start.4 = (bf16[1,256,2048]{2,1,0:T(8,128)(2,1)S(1)}, bf16[1,256,2048]{2,1,0:T(8,128)(2,1)}, u32[]{:S(2)}) copy-start(bf16[1,256,2048]{2,1,0:T(8,128)(2,1)} %param.8) | copy-start | bytes 3145732
  55.7 1.0 copy-start.1
  56.7 2.0 %copy-start.10 = (bf16[2,2048,512]{2,1,0:T(8,128)(2,1)}, bf16[2,2048,512]{2,1,0:T(8,128)(2,1)S(1)}, u32[]{:S(2)}) copy-start(bf16[2,2048,512]{2,1,0:T(8,128)(2,1)S(1)} %get-tuple-element.19.k_ref.v_ref) | copy-start | bytes 12582916
  84.6 1.0 copy-start.2
  85.6 1.1 copy-start.3

commit v3 on v2

v3 whole, which is shorter than its diff:
```python
import functools
import itertools
import math

import jax
import jax.numpy as jnp
from jax import lax
from jax.experimental import pallas as pl
from jax.experimental.pallas import tpu as pltpu
from jax.sharding import PartitionSpec as P

QUERY_HEADS = 16
KV_HEADS = 4
GROUP = QUERY_HEADS // KV_HEADS
HEAD_DIM = 128
BLOCK = 128
SLOTS = 8
STEP = 4
SCALE = 1.0 / math.sqrt(HEAD_DIM)
BF16 = jnp.bfloat16
F32 = jnp.float32
LOG2E = math.log2(math.e)
MESH = pl.DeviceIdType.MESH


def dot(a, b, ca, cb):
    return lax.dot_general(a, b, (((ca,), (cb,)), ((), ())), preferred_element_type=F32)


def stack_heads(ref, i):
    rows = slice(i * BLOCK, (i + 1) * BLOCK)
    return jnp.concatenate(
        [ref[rows, h * HEAD_DIM : (h + 1) * HEAD_DIM] for h in range(GROUP)], axis=0
    )


def attention_kernel(
    list_ref, count_ref, q_ref, do_ref, k_ref, v_ref,
    att_ref, att_t_ref, dq_ref, dk_ref, dv_ref, dk_acc, dv_acc,
):
    cols = GROUP * BLOCK
    count = q_ref.shape[0] // BLOCK
    dk_acc[...] = jnp.zeros_like(dk_acc)
    dv_acc[...] = jnp.zeros_like(dv_acc)

    def slots(ns):
        key_pos = lax.broadcasted_iota(jnp.int32, (BLOCK, cols), 0)
        query_pos = lax.broadcasted_iota(jnp.int32, (BLOCK, cols), 1) % BLOCK
        rows, k_sel, v_sel, qs, dos = [], [], [], [], []
        for i, n in enumerate(ns):
            rows.append(
                [pl.ds(pl.multiple_of(list_ref[i, j] * BLOCK, BLOCK), BLOCK) for j in range(n)]
            )
            k_sel.append(jnp.concatenate([k_ref[0, r, :] for r in rows[i]], axis=0))
            v_sel.append(jnp.concatenate([v_ref[0, r, :] for r in rows[i]], axis=0))
            qs.append(stack_heads(q_ref, i))
            dos.append(stack_heads(do_ref, i))
        scores = [dot(k, q, 1, 1) for k, q in zip(k_sel, qs)]
        prob_grads = [dot(v, do, 1, 1) for v, do in zip(v_sel, dos)]
        probs, rounded = [], []
        for i, (s, n) in enumerate(zip(scores, ns)):
            parts = [jnp.where(key_pos <= query_pos, s[:BLOCK], -1e30)]
            if n > STEP:
                parts.append(s[BLOCK : (n - STEP + 1) * BLOCK])
            for j in range(n - STEP + 1, n):
                dead = jnp.where(j < count_ref[i], 0.0, -1e30).astype(F32)
                parts.append(s[j * BLOCK : (j + 1) * BLOCK] + dead)
            s = jnp.concatenate(parts, axis=0)
            top = jnp.max(s, axis=0, keepdims=True)
            e = jnp.exp2((s - top) * (SCALE * LOG2E))
            p = e * (1.0 / jnp.sum(e, axis=0, keepdims=True))
            probs.append(p)
            rounded.append(p.astype(BF16))
        outs = [dot(v, pb, 0, 0).astype(BF16) for v, pb in zip(v_sel, rounded)]
        row_dots = [
            jnp.sum(o.astype(F32) * do.T.astype(F32), axis=0, keepdims=True)
            for o, do in zip(outs, dos)
        ]
        grads = [
            (p * (dp - r)).astype(BF16) for p, dp, r in zip(probs, prob_grads, row_dots)
        ]
        dqs = [(dot(k, ds, 0, 0) * SCALE).astype(BF16).T for k, ds in zip(k_sel, grads)]
        dks = [dot(ds, q, 1, 0) for ds, q in zip(grads, qs)]
        dvs = [dot(pb, do, 1, 0) for pb, do in zip(rounded, dos)]
        for i, (o_t, dq) in enumerate(zip(outs, dqs)):
            o = o_t.T
            mine = slice(i * BLOCK, (i + 1) * BLOCK)
            for h in range(GROUP):
                lanes = slice(h * HEAD_DIM, (h + 1) * HEAD_DIM)
                here = slice(h * BLOCK, (h + 1) * BLOCK)
                att_ref[mine, lanes] = o[here]
                dq_ref[mine, lanes] = dq[here]
                att_t_ref[h, :, mine] = o_t[:, here]
        for i, n in enumerate(ns):
            for j in range(n):
                here = slice(j * BLOCK, (j + 1) * BLOCK)
                dk_acc[rows[i][j], :] += dks[i][here]
                dv_acc[rows[i][j], :] += dvs[i][here]

    need = [(count_ref[i] + STEP - 1) // STEP for i in range(count)]
    for ns in itertools.product(range(STEP, SLOTS + 1, STEP), repeat=count):
        hit = functools.reduce(
            jnp.logical_and, [have == n // STEP for have, n in zip(need, ns)]
        )
        pl.when(hit)(functools.partial(slots, ns))

    dk_ref[...] = (dk_acc[...] * SCALE).astype(BF16)
    dv_ref[...] = dv_acc[...].astype(BF16)


def attention(queries, datt, kv, block_list, block_count):
    rows, width = queries.shape
    seq = kv.shape[1]
    group_cols = GROUP * HEAD_DIM
    kv_cols = KV_HEADS * HEAD_DIM
    q_spec = pl.BlockSpec((rows, group_cols), lambda g, *_: (0, g))

    def kv_spec(which):
        return pl.BlockSpec((1, seq, HEAD_DIM), lambda g, *_: (which, 0, g))

    out_spec = pl.BlockSpec((seq, HEAD_DIM), lambda g, *_: (0, g))
    t_spec = pl.BlockSpec((GROUP, HEAD_DIM, rows), lambda g, *_: (g, 0, 0))
    flops = 12 * rows * QUERY_HEADS * SLOTS * BLOCK * HEAD_DIM
    return pl.pallas_call(
        attention_kernel,
        grid_spec=pltpu.PrefetchScalarGridSpec(
            num_scalar_prefetch=2,
            grid=(KV_HEADS,),
            in_specs=[q_spec, q_spec, kv_spec(0), kv_spec(1)],
            out_specs=[q_spec, t_spec, q_spec, out_spec, out_spec],
            scratch_shapes=[pltpu.VMEM((seq, HEAD_DIM), F32)] * 2,
        ),
        out_shape=[
            jax.ShapeDtypeStruct((rows, width), BF16),
            jax.ShapeDtypeStruct((QUERY_HEADS, HEAD_DIM, rows), BF16),
            jax.ShapeDtypeStruct((rows, width), BF16),
            jax.ShapeDtypeStruct((seq, kv_cols), BF16),
            jax.ShapeDtypeStruct((seq, kv_cols), BF16),
        ],
        compiler_params=pltpu.CompilerParams(
            dimension_semantics=("arbitrary",), vmem_limit_bytes=60 << 20
        ),
        cost_estimate=pl.CostEstimate(
            flops=flops, bytes_accessed=12 << 20, transcendentals=rows * QUERY_HEADS * SLOTS * BLOCK
        ),
        name="attention",
    )(block_list, block_count, queries, datt, kv, kv)


def mesh_spot():
    c, f = lax.axis_index("ctx"), lax.axis_index("fsdp")
    return c, f, c // 2, lax.rem(c, 2), f // 4, lax.rem(f // 2, 2), lax.rem(f, 2)


def neighbours():
    c, f, z, xh, y, xl, k = mesh_spot()
    z_up, z_down = lax.rem(z + 1, 4), lax.rem(z + 3, 4)
    y_up, y_down = lax.rem(y + 1, 4), lax.rem(y + 3, 4)
    side, far, twin = 4 * y + 2 * (1 - xl) + k, 2 * z + 1 - xh, 4 * y + 2 * xl + 1 - k
    return dict(
        far=(far, f),
        near=(c, side),
        back=(far, side),
        twin=(c, twin),
        z_up=(2 * z_up + xh, f),
        z_down=(2 * z_down + xh, f),
        y_up=(c, 4 * y_up + 2 * xl + k),
        y_down=(c, 4 * y_down + 2 * xl + k),
    )


def meet(peers):
    barrier = pltpu.get_barrier_semaphore()
    for peer in peers:
        pl.semaphore_signal(barrier, inc=1, device_id=peer, device_id_type=MESH)
    pl.semaphore_wait(barrier, len(peers))


class Flows:
    def __init__(self, send_sem, recv_sem):
        self.send_sem, self.recv_sem, self.made = send_sem, recv_sem, []

    def send(self, src, dst, peer):
        n = len(self.made)
        copy = pltpu.make_async_remote_copy(
            src_ref=src,
            dst_ref=dst,
            send_sem=self.send_sem.at[n],
            recv_sem=self.recv_sem.at[n],
            device_id=peer,
            device_id_type=MESH,
        )
        copy.start()
        self.made.append(copy)
        return copy

    def finish(self):
        for copy in self.made:
            copy.wait_send()


GATHER_FLOWS = 40


def gather_kernel(
    keys, values, grad, w, kv, w_all, datt, grad_twin, w_buf, total, send_sem, recv_sem, here_sem
):
    c, f, z, xh, y, xl, k = mesh_spot()
    at = neighbours()
    z_up, z_down, z_far = lax.rem(z + 1, 4), lax.rem(z + 3, 4), lax.rem(z + 2, 4)
    y_up, y_down, y_far = lax.rem(y + 1, 4), lax.rem(y + 3, 4), lax.rem(y + 2, 4)
    rows = keys.shape[0]
    half = w.shape[0] // 2
    meet(list(at.values()))
    flows = Flows(send_sem, recv_sem)

    def chunk(a, who):
        return kv.at[a, pl.ds(pl.multiple_of(who * rows, rows), rows), :]

    def shard(yy, xx, kk):
        return 4 * yy + 2 * xx + kk

    def whole(who):
        return w_buf.at[who]

    def part(who, p):
        return w_buf.at[who, pl.ds(p * half, half), :]

    own = (keys, values)
    w_side = [
        flows.send(w.at[pl.ds(p * half, half), :], part(f, p), at[("near", "back")[p]])
        for p in (0, 1)
    ]
    w_up = flows.send(w, whole(f), at["y_up"])
    w_down = flows.send(w, whole(f), at["y_down"])
    kv_up = [flows.send(own[a], chunk(a, c), at["z_up"]) for a in (0, 1)]
    kv_down = [flows.send(own[a], chunk(a, c), at["z_down"]) for a in (1, 0)][::-1]
    kv_far = [flows.send(own[a], chunk(a, c), at["far"]) for a in (0, 1)]
    to_twin = [flows.send(w, whole(f), at["twin"])]
    swap = flows.send(grad, grad_twin, at["twin"])
    here = [
        pltpu.make_async_copy(keys, chunk(0, c), here_sem.at[0]),
        pltpu.make_async_copy(values, chunk(1, c), here_sem.at[1]),
        pltpu.make_async_copy(w, whole(f), here_sem.at[2]),
    ]
    for copy in here:
        copy.start()

    side = shard(y, 1 - xl, k)
    side_up, side_down = [], []

    def pass_side(p):
        w_side[p].wait_recv()
        side_up.append(flows.send(part(side, p), part(side, p), at["y_up"]))
        side_down.append(flows.send(part(side, p), part(side, p), at["y_down"]))

    pass_side(0)
    kv_up[0].wait_recv()
    got_k = 2 * z_down + xh
    on_k = flows.send(chunk(0, got_k), chunk(0, got_k), at["z_up"])
    kv_down[1].wait_recv()
    got_v = 2 * z_up + xh
    on_v = flows.send(chunk(1, got_v), chunk(1, got_v), at["z_down"])
    w_up.wait_recv()
    got = shard(y_down, xl, k)
    on_w0 = flows.send(part(got, 0), part(got, 0), at["y_up"])
    to_twin.append(flows.send(whole(got), whole(got), at["twin"]))
    w_down.wait_recv()
    got = shard(y_up, xl, k)
    on_w1 = flows.send(part(got, 1), part(got, 1), at["y_down"])
    to_twin.append(flows.send(whole(got), whole(got), at["twin"]))
    pass_side(1)
    to_twin.append(flows.send(whole(side), whole(side), at["twin"]))

    other = 2 * z + 1 - xh
    pair_up, pair_down = [None, None], [None, None]
    for a in (0, 1):
        kv_far[a].wait_recv()
        pair_up[a] = flows.send(chunk(a, other), chunk(a, other), at["z_up"])
        pair_down[a] = flows.send(chunk(a, other), chunk(a, other), at["z_down"])

    def multiply(yy, n):
        slab = pl.ds(pl.multiple_of(4 * yy, 4), 4)
        out = pltpu.make_async_copy(w_buf.at[slab], w_all.at[slab], here_sem.at[3 + n])
        out.start()
        here.append(out)

        def columns(b, carry):
            lanes = pl.ds(pl.multiple_of(b * 512, 512), 512)
            out = None
            for s in range(4):
                who = 4 * yy + s
                g = grad[:, pl.ds(pl.multiple_of(who * HEAD_DIM, HEAD_DIM), HEAD_DIM)]
                term = dot(g, w_buf[who, lanes, :], 1, 1)
                out = term if out is None else out + term
            total[:, lanes] = out if n == 0 else total[:, lanes] + out
            return carry

        lax.fori_loop(0, total.shape[1] // 512, columns, 0)

    here.pop().wait()
    for n in (0, 3):
        to_twin[n].wait_recv()
    multiply(y, 0)

    def piece(a, who, p):
        start = pl.multiple_of(who * rows, rows) + p * (rows // 2)
        return kv.at[a, pl.ds(start, rows // 2), :]

    on_k.wait_recv()
    got = 2 * z_far + xh
    cross_k = flows.send(piece(0, got, 1), piece(0, got, 1), at["far"])
    on_v.wait_recv()
    cross_v = flows.send(piece(1, got, 1), piece(1, got, 1), at["far"])
    got = shard(y_far, xl, k)
    on_w0.wait_recv()
    on_s0 = flows.send(part(got, 0), part(got, 0), at["near"])
    to_twin.append(flows.send(part(got, 0), part(got, 0), at["twin"]))
    on_w1.wait_recv()
    on_s1 = flows.send(part(got, 1), part(got, 1), at["back"])
    to_twin.append(flows.send(part(got, 1), part(got, 1), at["twin"]))

    pair_up[0].wait_recv()
    got = 2 * z_down + 1 - xh
    pair_on_k = flows.send(piece(0, got, 0), piece(0, got, 0), at["z_up"])
    pair_down[1].wait_recv()
    got = 2 * z_up + 1 - xh
    pair_on_v = flows.send(piece(1, got, 0), piece(1, got, 0), at["z_down"])

    for yy, arrived in ((y_down, side_up), (y_up, side_down)):
        got = shard(yy, 1 - xl, k)
        for copy in arrived:
            copy.wait_recv()
        to_twin.append(flows.send(whole(got), whole(got), at["twin"]))
    got = shard(y_far, 1 - xl, k)
    on_s0.wait_recv()
    to_twin.append(flows.send(part(got, 0), part(got, 0), at["twin"]))
    on_s1.wait_recv()
    to_twin.append(flows.send(part(got, 1), part(got, 1), at["twin"]))
    for n in (1, 6):
        to_twin[n].wait_recv()
    multiply(y_down, 1)
    for n in (2, 7):
        to_twin[n].wait_recv()
    multiply(y_up, 2)
    for n in (4, 5, 8, 9):
        to_twin[n].wait_recv()
    multiply(y_far, 3)
    datt[...] = total[...].astype(BF16)
    for copy in (swap, kv_up[1], kv_down[0], pair_up[1], pair_down[0]):
        copy.wait_recv()
    for copy in (cross_k, cross_v, pair_on_k, pair_on_v):
        copy.wait_recv()
    flows.finish()
    for copy in here:
        copy.wait()


def gather(keys, values, grad, w):
    rows, kv_cols = keys.shape
    feats, cols = w.shape
    n_ctx, n_fsdp = lax.axis_size("ctx"), lax.axis_size("fsdp")
    hbm = pl.BlockSpec(memory_space=pltpu.HBM)
    vmem = pl.BlockSpec(memory_space=pltpu.VMEM)
    return pl.pallas_call(
        gather_kernel,
        in_specs=[hbm, hbm, vmem, hbm],
        out_specs=[hbm, hbm, vmem, hbm],
        out_shape=[
            jax.ShapeDtypeStruct((2, n_ctx * rows, kv_cols), BF16),
            jax.ShapeDtypeStruct((n_fsdp, feats, cols), BF16),
            jax.ShapeDtypeStruct((rows, feats), BF16),
            jax.ShapeDtypeStruct(grad.shape, BF16),
        ],
        scratch_shapes=[
            pltpu.VMEM((n_fsdp, feats, cols), BF16),
            pltpu.VMEM((rows, feats), F32),
            pltpu.SemaphoreType.DMA((GATHER_FLOWS,)),
            pltpu.SemaphoreType.DMA((GATHER_FLOWS,)),
            pltpu.SemaphoreType.DMA((7,)),
        ],
        compiler_params=pltpu.CompilerParams(
            collective_id=0, has_side_effects=True, vmem_limit_bytes=60 << 20
        ),
        cost_estimate=pl.CostEstimate(
            flops=2 * rows * feats * feats, bytes_accessed=24 << 20, transcendentals=0
        ),
        name="gather",
    )(keys, values, grad, w)


REDUCE_FLOWS = 66
PIECES = 2
PARTS = 4
PART_ROWS = 2 * HEAD_DIM // PARTS


def reduce_kernel(
    dk, dv, att, att_t, grad, grad_twin, resid, w_all,
    mixed, dk_out, dv_out, proj,
    att_twin, w_buf, att_buf, res_buf, ahead, mine, hop_in, raw_in, sum_in, sum_out, kept, far_out, far_in,
    far_p, own_keep, up_raw, down_raw, top_in, low_in, top_out, low_out,
    top_raw, low_raw, top_sum, low_sum, x_out, x_in, x_keep, z_out, z_in,
    send_sem, recv_sem, here_sem,
):
    c, f, z, xh, y, xl, k = mesh_spot()
    at = neighbours()
    z_up, z_down, z_far = lax.rem(z + 1, 4), lax.rem(z + 3, 4), lax.rem(z + 2, 4)
    y_up, y_down, y_far = lax.rem(y + 1, 4), lax.rem(y + 3, 4), lax.rem(y + 2, 4)
    at["z_far"] = (2 * z_far + xh, f)
    rows, kv_cols = dk_out.shape
    pair = 2 * rows
    wide = kv_cols // PIECES
    meet(list(at.values()))
    flows = Flows(send_sem, recv_sem)
    parts = (dk, dv)

    def block(a, zz, p):
        return parts[a].at[
            pl.ds(pl.multiple_of(zz * pair, pair), pair), pl.ds(p * wide, wide)
        ]

    swap = flows.send(att_t, att_twin, at["twin"])
    hops = [
        [
            flows.send(block(0, z_far, p), hop_in.at[0, p], at["z_up"]),
            flows.send(block(1, z_far, p), hop_in.at[1, p], at["z_down"]),
        ]
        for p in range(PIECES)
    ]
    here = []
    for n, (src, dst) in enumerate(
        [
            (dk.at[pl.ds(pl.multiple_of(z_up * pair, pair), pair), :], ahead.at[0]),
            (dv.at[pl.ds(pl.multiple_of(z_down * pair, pair), pair), :], ahead.at[1]),
            (dk.at[pl.ds(pl.multiple_of(z * pair, pair), pair), :], mine.at[0]),
            (dv.at[pl.ds(pl.multiple_of(z * pair, pair), pair), :], mine.at[1]),
            (w_all, w_buf),
            (att, att_buf),
            (resid, res_buf),
        ]
    ):
        copy = pltpu.make_async_copy(src, dst, here_sem.at[n])
        copy.start()
        here.append(copy)

    def product(yy, p, low):
        lanes = [
            pl.ds(pl.multiple_of((4 * yy + 2 * s + k) * HEAD_DIM, HEAD_DIM), HEAD_DIM)
            for s in (0, 1)
        ]
        first, of = p % (PARTS // 2) * PART_ROWS, p // (PARTS // 2)

        def term(left, right):
            heads = [left[2 * (m + low) + of, first : first + PART_ROWS] for m in range(4)]
            wide = jnp.concatenate([right[:, s] for s in lanes], axis=1)
            return dot(jnp.concatenate(heads, axis=0), wide, 1, 0)

        out = term(att_t, grad) + term(att_twin, grad_twin)
        return out.reshape(4, PART_ROWS, 2 * HEAD_DIM)

    swap.wait_recv()
    top_hop, low_hop = [], []
    for p in range(PARTS):
        far_p[p, 0:4] = product(y_far, p, 0).astype(BF16)
        top_hop.append(flows.send(far_p.at[p, pl.ds(0, 4)], top_in.at[p], at["y_up"]))
        far_p[p, 4:8] = product(y_far, p, 4).astype(BF16)
        low_hop.append(flows.send(far_p.at[p, pl.ds(4, 4)], low_in.at[p], at["y_down"]))
    for copy in here[:4]:
        copy.wait()
    raws, sums = [], []
    raw_top, raw_low, top_on, low_on = [], [], [], []

    def relay_kv(p):
        cols = slice(p * wide, (p + 1) * wide)
        raws.append(
            [
                flows.send(block(0, z_down, p), raw_in.at[0, p], at["z_down"]),
                flows.send(block(1, z_up, p), raw_in.at[1, p], at["z_up"]),
            ]
        )
        sums.append([])
        for a, towards in ((0, "z_up"), (1, "z_down")):
            hops[p][a].wait_recv()
            sum_out[a, p] = (ahead[a, :, cols].astype(F32) + hop_in[a, p].astype(F32)).astype(BF16)
            sums[p].append(flows.send(sum_out.at[a, p], sum_in.at[a, p], at[towards]))

    for p in range(PARTS):
        up_raw[p] = product(y_up, p, 4).astype(BF16)
        raw_low.append(flows.send(up_raw.at[p], low_raw.at[p], at["y_up"]))
        down_raw[p] = product(y_down, p, 0).astype(BF16)
        raw_top.append(flows.send(down_raw.at[p], top_raw.at[p], at["y_down"]))
        keep = product(y_up, p, 0)
        top_hop[p].wait_recv()
        top_out[p] = (keep + top_in[p].astype(F32)).astype(BF16)
        top_on.append(flows.send(top_out.at[p], top_sum.at[p], at["y_up"]))
        keep = product(y_down, p, 4)
        low_hop[p].wait_recv()
        low_out[p] = (keep + low_in[p].astype(F32)).astype(BF16)
        low_on.append(flows.send(low_out.at[p], low_sum.at[p], at["y_down"]))
        if p % 2:
            relay_kv(p // 2)
    for p in range(PARTS):
        own_keep[p, 0:4] = product(y, p, 0)
        own_keep[p, 4:8] = product(y, p, 4)

    for copy in here[4:]:
        copy.wait()

    def project(n, carry):
        lanes = pl.ds(pl.multiple_of(n * HEAD_DIM, HEAD_DIM), HEAD_DIM)
        out = dot(att_buf[...], w_buf[n], 1, 0)
        mixed[:, lanes] = (res_buf[:, lanes].astype(F32) + out).astype(BF16)
        return carry

    def mix(quarter):
        many = w_buf.shape[0] // 4
        lax.fori_loop(quarter * many, (quarter + 1) * many, project, 0)

    keep_rows = pl.ds(pl.multiple_of(xh * rows, rows), rows)
    give_rows = pl.ds(pl.multiple_of((1 - xh) * rows, rows), rows)
    fars, x_flow, z_flow = [], [], []
    x_to = ("near", "far", "back")
    z_to = (("z_up", z_up), ("z_down", z_down), ("z_far", z_far))
    near_lanes = pl.ds(pl.multiple_of((1 - xl) * HEAD_DIM, HEAD_DIM), HEAD_DIM)
    own_lanes = pl.ds(pl.multiple_of(xl * HEAD_DIM, HEAD_DIM), HEAD_DIM)

    def cross_kv(p):
        cols = pl.ds(p * wide, wide)
        fars.append([])
        for a in (0, 1):
            raws[p][a].wait_recv()
            sums[p][a].wait_recv()

            def gathered(which):
                return (
                    mine[a, which, cols].astype(F32)
                    + raw_in[a, p, which, :].astype(F32)
                    + sum_in[a, p, which, :].astype(F32)
                )

            far_out[a, p] = gathered(give_rows).astype(BF16)
            fars[p].append(flows.send(far_out.at[a, p], far_in.at[a, p], at["far"]))
            kept[a, p] = gathered(keep_rows)

    def cross(p):
        raw_top[p].wait_recv()
        top_on[p].wait_recv()
        raw_low[p].wait_recv()
        low_on[p].wait_recv()
        for m in range(4):
            own_keep[p, m] += top_raw[p, m].astype(F32) + top_sum[p, m].astype(F32)
            own_keep[p, m + 4] += low_raw[p, m].astype(F32) + low_sum[p, m].astype(F32)
        sent = []
        for n, (hi, lanes) in enumerate(
            ((xh, near_lanes), (1 - xh, own_lanes), (1 - xh, near_lanes))
        ):
            for zz in range(4):
                x_out[p, n, zz] = own_keep[p, 2 * zz + hi, :, lanes].astype(BF16)
            sent.append(flows.send(x_out.at[p, n], x_in.at[p, n], at[x_to[n]]))
        x_flow.append(sent)

    def along(p):
        for n in range(3):
            x_flow[p][n].wait_recv()
        for zz in range(4):
            total = own_keep[p, 2 * zz + xh, :, own_lanes]
            for n in range(3):
                total += x_in[p, n, zz].astype(F32)
            x_keep[p, zz] = total
        sent = []
        for n, (name, zz) in enumerate(z_to):
            z_out[p, n] = x_keep[p, zz].astype(BF16)
            sent.append(flows.send(z_out.at[p, n], z_in.at[p, n], at[name]))
        z_flow.append(sent)

    def finish_kv(p):
        cols = slice(p * wide, (p + 1) * wide)
        for a, out in ((0, dk_out), (1, dv_out)):
            fars[p][a].wait_recv()
            out[:, cols] = (kept[a, p] + far_in[a, p].astype(F32)).astype(BF16)

    mix(0)
    mix(1)
    cross(0)
    cross_kv(0)
    mix(2)
    cross(1)
    along(0)
    mix(3)
    cross(2)
    along(1)
    cross_kv(1)
    finish_kv(0)
    cross(3)
    along(2)
    finish_kv(1)
    along(3)
    for p in range(PARTS):
        total = x_keep[p, z]
        for n in range(3):
            z_flow[p][n].wait_recv()
            total += z_in[p, n].astype(F32)
        proj[p * PART_ROWS : (p + 1) * PART_ROWS, :] = total
    flows.finish()


def reduce(dk, dv, att, att_t, grad, grad_twin, resid, w_all):
    n_ctx = lax.axis_size("ctx")
    seq, kv_cols = dk.shape
    rows, feats = att.shape
    chunk = seq // n_ctx
    heads = att_t.shape[0]
    per = heads // n_ctx
    wide = kv_cols // PIECES
    hbm = pl.BlockSpec(memory_space=pltpu.HBM)
    vmem = pl.BlockSpec(memory_space=pltpu.VMEM)

    def quad(dtype, n=4, lanes=2 * HEAD_DIM):
        return pltpu.VMEM((PARTS, n, PART_ROWS, lanes), dtype)

    def kv_buf(height, dtype=BF16):
        return pltpu.VMEM((2, PIECES, height, wide), dtype)

    return pl.pallas_call(
        reduce_kernel,
        in_specs=[hbm, hbm, hbm, vmem, vmem, vmem, hbm, hbm],
        out_specs=[vmem] * 4,
        out_shape=[
            jax.ShapeDtypeStruct((rows, feats), BF16),
            jax.ShapeDtypeStruct((chunk, kv_cols), BF16),
            jax.ShapeDtypeStruct((chunk, kv_cols), BF16),
            jax.ShapeDtypeStruct((per * HEAD_DIM, HEAD_DIM), F32),
        ],
        scratch_shapes=[
            pltpu.VMEM(att_t.shape, BF16),
            pltpu.VMEM(w_all.shape, BF16),
            pltpu.VMEM(att.shape, BF16),
            pltpu.VMEM(resid.shape, BF16),
            pltpu.VMEM((2, 2 * chunk, kv_cols), BF16),
            pltpu.VMEM((2, 2 * chunk, kv_cols), BF16),
            kv_buf(2 * chunk),
            kv_buf(2 * chunk),
            kv_buf(2 * chunk),
            kv_buf(2 * chunk),
            kv_buf(chunk, F32),
            kv_buf(chunk),
            kv_buf(chunk),
            quad(BF16, 8),
            quad(F32, 8),
            quad(BF16),
            quad(BF16),
            quad(BF16),
            quad(BF16),
            quad(BF16),
            quad(BF16),
            quad(BF16),
            quad(BF16),
            quad(BF16),
            quad(BF16),
            pltpu.VMEM((PARTS, 3, 4, PART_ROWS, HEAD_DIM), BF16),
            pltpu.VMEM((PARTS, 3, 4, PART_ROWS, HEAD_DIM), BF16),
            quad(F32, 4, HEAD_DIM),
            quad(BF16, 3, HEAD_DIM),
            quad(BF16, 3, HEAD_DIM),
            pltpu.SemaphoreType.DMA((REDUCE_FLOWS,)),
            pltpu.SemaphoreType.DMA((REDUCE_FLOWS,)),
            pltpu.SemaphoreType.DMA((7,)),
        ],
        compiler_params=pltpu.CompilerParams(
            collective_id=1, has_side_effects=True, vmem_limit_bytes=50 << 20
        ),
        cost_estimate=pl.CostEstimate(
            flops=4 * rows * feats * feats, bytes_accessed=24 << 20, transcendentals=0
        ),
        name="reduce",
    )(dk, dv, att, att_t, grad, grad_twin, resid, w_all)


def local(queries, keys, values, resid, grad_out, w_out, block_list, block_count):
    grad = grad_out[0]
    kv, w_all, datt, grad_twin = gather(keys[0], values[0], grad, w_out)
    att, att_t, dq, dk, dv = attention(queries[0], datt, kv, block_list, block_count)
    mixed, dk, dv, proj = reduce(dk, dv, att, att_t, grad, grad_twin, resid[0], w_all)
    return mixed[None], dq[None], dk[None], dv[None], proj


def solution(mesh):
    rows = P("fsdp", "ctx", None)
    in_specs = (rows, rows, rows, rows, rows, P(None, "fsdp"), P("ctx", None), P("ctx"))
    out_specs = (rows, rows, rows, rows, P("ctx", "fsdp"))
    return jax.shard_map(local, mesh=mesh, in_specs=in_specs, out_specs=out_specs, check_vma=False)
```

time: 154 us -> 133 us (0.86)
  Pallas kernels: 141 us -> 126 us
  local copies, waits for them, and re-layouts: 12.2 us -> 5.48 us
    pallas_call x1, Pallas kernels: 25.9 us -> 13.8 us  [attention(): pl.pallas_call(attention_kernel, grid_spec=pltpu.PrefetchScalarGridSpec(n...]
    unnamed x26 -> x8, local copies, waits for them, and re-layouts: 12.2 us -> 5.48 us
    pallas_call x1, Pallas kernels: 50.9 us -> 49.2 us  [gather(): pl.pallas_call(gather_kernel, in_specs=[hbm, hbm, vmem, hbm], out_specs=[...]
where the time goes in v3:
time: 133 us; the launch traced here: 132 us
  Pallas kernels  126 us (95%)
  local copies, waits for them, and re-layouts  5.48 us (4%)
    pallas_call x1, Pallas kernels, reduce(): pl.pallas_call(reduce_kernel, in_specs=[hbm, hbm, hbm, vmem, vmem, vmem,...  63 us
    pallas_call x1, Pallas kernels, gather(): pl.pallas_call(gather_kernel, in_specs=[hbm, hbm, vmem, hbm], out_specs=[...  49.2 us
    pallas_call x1, Pallas kernels, attention(): pl.pallas_call(attention_kernel, grid_spec=pltpu.PrefetchScalarGridSpec(n...  13.8 us
    unnamed x8, local copies, waits for them, and re-layouts  5.48 us

profile of v3, /device:TPU:0, one launch (start us, length us, event | category | flops | bytes accessed | tf_op | source)
XLA Modules:
  0.0 132.1 jit_solution(6690659656173658197)
XLA Ops:
  0.6 49.2 %gather.1 = (bf16[2,2048,512]{2,1,0:T(8,128)(2,1)}, bf16[16,2048,128]{2,1,0:T(8,128)(2,1)}, bf16[256,2048]{1,0:T(8,128)(2,1)}, bf16[256,2048]{1,0:T(8,128)(2,1)}) custom-call(bf16[256,512]{1,0:T(8,128)(2,1)} %bitcast.16, bf16[256,512]{1,0:T(8,128)(2,1)} %bitcast.17, bf16[256,2048]{1,0:T(8,128)(2,1)} %bitcast.12, bf16[2048,128]{1,0:T(8,128)(2,1)} %w.1), custom_call_target="tpu_custom_call" | custom-call | flops 2147483648 | bytes 25165824 | tf_op jit(solution)/shard_map/gather/pallas_call | solution.py:365
  49.8 13.8 %attention.1 = (bf16[256,2048]{1,0:T(8,128)(2,1)}, bf16[16,128,256]{2,1,0:T(8,128)(2,1)}, bf16[256,2048]{1,0:T(8,128)(2,1)}, bf16[2048,512]{1,0:T(8,128)(2,1)}, bf16[2048,512]{1,0:T(8,128)(2,1)}) custom-call(s32[2,8]{1,0:T(2,128)} %list_ref.1, s32[2]{0:T(128)} %count_ref.1, bf16[256,2048]{1,0:T(8,128)(2,1)} %bitcast.15, ...), custom_call_target="tpu_custom_call" | custom-call | flops 6442450944 | bytes 12582912 | tf_op jit(solution)/shard_map/attention/pallas_call | solution.py:124
  63.6 0.0 copy-start
  63.6 1.2 copy-done
  64.9 0.0 copy-start.1
  64.9 1.2 copy-done.1
  66.1 63.0 %reduce.1 = (bf16[256,2048]{1,0:T(8,128)(2,1)S(1)}, bf16[256,512]{1,0:T(8,128)(2,1)S(1)}, bf16[256,512]{1,0:T(8,128)(2,1)S(1)}, f32[256,128]{1,0:T(8,128)S(1)}) custom-call(bf16[2048,512]{1,0:T(8,128)(2,1)} %get-tuple-element.20.dk, bf16[2048,512]{1,0:T(8,128)(2,1)} %get-tuple-element.21.dv, bf16[256,2048]{1,0:T(8,128)(2,1)S(1)} %copy-done, ...), custom_call_target="tpu_custom_call" | custom-call | flops 4294967296 | bytes 25165824 | tf_op jit(solution)/shard_map/reduce/pallas_call | solution.py:625
  129.0 1.0 copy.17
  130.0 0.7 copy.18
  130.7 0.7 copy.19
  131.4 0.7 copy.20
Async XLA Ops:
  63.6 1.2 copy-start
  64.9 1.2 copy-start.1

commit v4 on v3

--- a/solution.py
+++ b/solution.py
@@ -138,7 +138,7 @@
             jax.ShapeDtypeStruct((seq, kv_cols), BF16),
         ],
         compiler_params=pltpu.CompilerParams(
-            dimension_semantics=("arbitrary",), vmem_limit_bytes=60 << 20
+            dimension_semantics=("arbitrary",), vmem_limit_bytes=44 << 20
         ),
         cost_estimate=pl.CostEstimate(
             flops=flops, bytes_accessed=12 << 20, transcendentals=rows * QUERY_HEADS * SLOTS * BLOCK
@@ -176,11 +176,32 @@
     pl.semaphore_wait(barrier, len(peers))
 
 
+def act_if(condition, act):
+    def run():
+        act()
+
+    if condition is None:
+        run()
+    else:
+        pl.when(condition)(run)
+
+
+class Sent:
+    def __init__(self, copy, gives, takes):
+        self.copy, self.gives, self.takes = copy, gives, takes
+
+    def wait_recv(self):
+        act_if(self.takes, self.copy.wait_recv)
+
+    def wait_send(self):
+        act_if(self.gives, self.copy.wait_send)
+
+
 class Flows:
     def __init__(self, send_sem, recv_sem):
         self.send_sem, self.recv_sem, self.made = send_sem, recv_sem, []
 
-    def send(self, src, dst, peer):
+    def send(self, src, dst, peer, gives=None, takes=None):
         n = len(self.made)
         copy = pltpu.make_async_remote_copy(
             src_ref=src,
@@ -190,9 +211,9 @@
             device_id=peer,
             device_id_type=MESH,
         )
-        copy.start()
-        self.made.append(copy)
-        return copy
+        act_if(gives, copy.start)
+        self.made.append(Sent(copy, gives, takes))
+        return self.made[-1]
 
     def finish(self):
         for copy in self.made:
@@ -227,14 +248,19 @@
         return w_buf.at[who, pl.ds(p * half, half), :]
 
     own = (keys, values)
+    up = dict(gives=z < 3, takes=z_down < 3)
+    down = (dict(gives=z < 1, takes=z_up < 1), dict(gives=z < 2, takes=z_up < 2))
+    on_up = dict(gives=(z == 1) | (z == 2), takes=z >= 2)
+    on_down = dict(gives=(z == 0) | (z == 3), takes=z >= 2)
+    later = dict(gives=z >= 2, takes=z >= 2)
     w_side = [
         flows.send(w.at[pl.ds(p * half, half), :], part(f, p), at[("near", "back")[p]])
         for p in (0, 1)
     ]
     w_up = flows.send(w, whole(f), at["y_up"])
     w_down = flows.send(w, whole(f), at["y_down"])
-    kv_up = [flows.send(own[a], chunk(a, c), at["z_up"]) for a in (0, 1)]
-    kv_down = [flows.send(own[a], chunk(a, c), at["z_down"]) for a in (1, 0)][::-1]
+    kv_up = [flows.send(own[a], chunk(a, c), at["z_up"], **up) for a in (0, 1)]
+    kv_down = [flows.send(own[a], chunk(a, c), at["z_down"], **down[a]) for a in (1, 0)][::-1]
     kv_far = [flows.send(own[a], chunk(a, c), at["far"]) for a in (0, 1)]
     to_twin = [flows.send(w, whole(f), at["twin"])]
     swap = flows.send(grad, grad_twin, at["twin"])
@@ -257,10 +283,10 @@
     pass_side(0)
     kv_up[0].wait_recv()
     got_k = 2 * z_down + xh
-    on_k = flows.send(chunk(0, got_k), chunk(0, got_k), at["z_up"])
+    on_k = flows.send(chunk(0, got_k), chunk(0, got_k), at["z_up"], **on_up)
     kv_down[1].wait_recv()
     got_v = 2 * z_up + xh
-    on_v = flows.send(chunk(1, got_v), chunk(1, got_v), at["z_down"])
+    on_v = flows.send(chunk(1, got_v), chunk(1, got_v), at["z_down"], **on_down)
     w_up.wait_recv()
     got = shard(y_down, xl, k)
     on_w0 = flows.send(part(got, 0), part(got, 0), at["y_up"])
@@ -276,8 +302,8 @@
     pair_up, pair_down = [None, None], [None, None]
     for a in (0, 1):
         kv_far[a].wait_recv()
-        pair_up[a] = flows.send(chunk(a, other), chunk(a, other), at["z_up"])
-        pair_down[a] = flows.send(chunk(a, other), chunk(a, other), at["z_down"])
+        pair_up[a] = flows.send(chunk(a, other), chunk(a, other), at["z_up"], **up)
+        pair_down[a] = flows.send(chunk(a, other), chunk(a, other), at["z_down"], **down[a])
 
     def multiply(yy, n):
         slab = pl.ds(pl.multiple_of(4 * yy, 4), 4)
@@ -288,10 +314,11 @@
         def columns(b, carry):
             lanes = pl.ds(pl.multiple_of(b * 512, 512), 512)
             out = None
-            for s in range(4):
+            for s in (0, 2):
                 who = 4 * yy + s
-                g = grad[:, pl.ds(pl.multiple_of(who * HEAD_DIM, HEAD_DIM), HEAD_DIM)]
-                term = dot(g, w_buf[who, lanes, :], 1, 1)
+                g = grad[:, pl.ds(pl.multiple_of(who * HEAD_DIM, 2 * HEAD_DIM), 2 * HEAD_DIM)]
+                both = jnp.concatenate([w_buf[who, lanes, :], w_buf[who + 1, lanes, :]], axis=1)
+                term = dot(g, both, 1, 1)
                 out = term if out is None else out + term
             total[:, lanes] = out if n == 0 else total[:, lanes] + out
             return carry
@@ -309,9 +336,9 @@
 
     on_k.wait_recv()
     got = 2 * z_far + xh
-    cross_k = flows.send(piece(0, got, 1), piece(0, got, 1), at["far"])
+    cross_k = flows.send(piece(0, got, 1), piece(0, got, 1), at["far"], **later)
     on_v.wait_recv()
-    cross_v = flows.send(piece(1, got, 1), piece(1, got, 1), at["far"])
+    cross_v = flows.send(piece(1, got, 1), piece(1, got, 1), at["far"], **later)
     got = shard(y_far, xl, k)
     on_w0.wait_recv()
     on_s0 = flows.send(part(got, 0), part(got, 0), at["near"])
@@ -322,10 +349,10 @@
 
     pair_up[0].wait_recv()
     got = 2 * z_down + 1 - xh
-    pair_on_k = flows.send(piece(0, got, 0), piece(0, got, 0), at["z_up"])
+    pair_on_k = flows.send(piece(0, got, 0), piece(0, got, 0), at["z_up"], **on_up)
     pair_down[1].wait_recv()
     got = 2 * z_up + 1 - xh
-    pair_on_v = flows.send(piece(1, got, 0), piece(1, got, 0), at["z_down"])
+    pair_on_v = flows.send(piece(1, got, 0), piece(1, got, 0), at["z_down"], **on_down)
 
     for yy, arrived in ((y_down, side_up), (y_up, side_down)):
         got = shard(yy, 1 - xl, k)
@@ -398,7 +425,7 @@
 def reduce_kernel(
     dk, dv, att, att_t, grad, grad_twin, resid, w_all,
     mixed, dk_out, dv_out, proj,
-    att_twin, w_buf, att_buf, res_buf, ahead, mine, hop_in, raw_in, sum_in, sum_out, kept, far_out, far_in,
+    att_twin, w_buf, res_buf, ahead, mine, hop_in, raw_in, sum_in, sum_out, kept, far_out, far_in,
     far_p, own_keep, up_raw, down_raw, top_in, low_in, top_out, low_out,
     top_raw, low_raw, top_sum, low_sum, x_out, x_in, x_keep, z_out, z_in,
     send_sem, recv_sem, here_sem,
@@ -421,10 +448,26 @@
         ]
 
     swap = flows.send(att_t, att_twin, at["twin"])
+    hop_in_k, hop_in_v = z_down >= 2, z_up >= 2
+    raw_in_k, raw_in_v = z_up >= 1, z_down == 3
+    sum_in_k, sum_in_v = (z_down == 3) | (z_down == 0), z_up >= 1
+    for buffer, a, comes in (
+        (hop_in, 0, hop_in_k),
+        (hop_in, 1, hop_in_v),
+        (raw_in, 0, raw_in_k),
+        (raw_in, 1, raw_in_v),
+        (sum_in, 0, sum_in_k),
+        (sum_in, 1, sum_in_v),
+    ):
+
+        def clear(buffer=buffer, a=a):
+            buffer[a] = jnp.zeros_like(buffer[a])
+
+        pl.when(jnp.logical_not(comes))(clear)
     hops = [
         [
-            flows.send(block(0, z_far, p), hop_in.at[0, p], at["z_up"]),
-            flows.send(block(1, z_far, p), hop_in.at[1, p], at["z_down"]),
+            flows.send(block(0, z_far, p), hop_in.at[0, p], at["z_up"], z >= 2, hop_in_k),
+            flows.send(block(1, z_far, p), hop_in.at[1, p], at["z_down"], z >= 2, hop_in_v),
         ]
         for p in range(PIECES)
     ]
@@ -436,7 +479,6 @@
             (dk.at[pl.ds(pl.multiple_of(z * pair, pair), pair), :], mine.at[0]),
             (dv.at[pl.ds(pl.multiple_of(z * pair, pair), pair), :], mine.at[1]),
             (w_all, w_buf),
-            (att, att_buf),
             (resid, res_buf),
         ]
     ):
@@ -475,15 +517,20 @@
         cols = slice(p * wide, (p + 1) * wide)
         raws.append(
             [
-                flows.send(block(0, z_down, p), raw_in.at[0, p], at["z_down"]),
-                flows.send(block(1, z_up, p), raw_in.at[1, p], at["z_up"]),
+                flows.send(block(0, z_down, p), raw_in.at[0, p], at["z_down"], z >= 1, raw_in_k),
+                flows.send(block(1, z_up, p), raw_in.at[1, p], at["z_up"], z == 3, raw_in_v),
             ]
         )
         sums.append([])
-        for a, towards in ((0, "z_up"), (1, "z_down")):
+        for a, towards, gives, takes in (
+            (0, "z_up", (z == 3) | (z == 0), sum_in_k),
+            (1, "z_down", z >= 1, sum_in_v),
+        ):
             hops[p][a].wait_recv()
             sum_out[a, p] = (ahead[a, :, cols].astype(F32) + hop_in[a, p].astype(F32)).astype(BF16)
-            sums[p].append(flows.send(sum_out.at[a, p], sum_in.at[a, p], at[towards]))
+            sums[p].append(
+                flows.send(sum_out.at[a, p], sum_in.at[a, p], at[towards], gives, takes)
+            )
 
     for p in range(PARTS):
         up_raw[p] = product(y_up, p, 4).astype(BF16)
@@ -508,13 +555,14 @@
         copy.wait()
 
     def project(n, carry):
-        lanes = pl.ds(pl.multiple_of(n * HEAD_DIM, HEAD_DIM), HEAD_DIM)
-        out = dot(att_buf[...], w_buf[n], 1, 0)
+        lanes = pl.ds(pl.multiple_of(n * 2 * HEAD_DIM, 2 * HEAD_DIM), 2 * HEAD_DIM)
+        both = jnp.concatenate([w_buf[2 * n], w_buf[2 * n + 1]], axis=1)
+        out = dot(att[...], both, 1, 0)
         mixed[:, lanes] = (res_buf[:, lanes].astype(F32) + out).astype(BF16)
         return carry
 
     def mix(quarter):
-        many = w_buf.shape[0] // 4
+        many = w_buf.shape[0] // 8
         lax.fori_loop(quarter * many, (quarter + 1) * many, project, 0)
 
     keep_rows = pl.ds(pl.multiple_of(xh * rows, rows), rows)
@@ -624,7 +672,7 @@
 
     return pl.pallas_call(
         reduce_kernel,
-        in_specs=[hbm, hbm, hbm, vmem, vmem, vmem, hbm, hbm],
+        in_specs=[hbm, hbm, vmem, vmem, vmem, vmem, hbm, hbm],
         out_specs=[vmem] * 4,
         out_shape=[
             jax.ShapeDtypeStruct((rows, feats), BF16),
@@ -635,7 +683,6 @@
         scratch_shapes=[
             pltpu.VMEM(att_t.shape, BF16),
             pltpu.VMEM(w_all.shape, BF16),
-            pltpu.VMEM(att.shape, BF16),
             pltpu.VMEM(resid.shape, BF16),
             pltpu.VMEM((2, 2 * chunk, kv_cols), BF16),
             pltpu.VMEM((2, 2 * chunk, kv_cols), BF16),
@@ -665,10 +712,10 @@
             quad(BF16, 3, HEAD_DIM),
             pltpu.SemaphoreType.DMA((REDUCE_FLOWS,)),
             pltpu.SemaphoreType.DMA((REDUCE_FLOWS,)),
-            pltpu.SemaphoreType.DMA((7,)),
+            pltpu.SemaphoreType.DMA((6,)),
         ],
         compiler_params=pltpu.CompilerParams(
-            collective_id=1, has_side_effects=True, vmem_limit_bytes=50 << 20
+            collective_id=1, has_side_effects=True, vmem_limit_bytes=40 << 20
         ),
         cost_estimate=pl.CostEstimate(
             flops=4 * rows * feats * feats, bytes_accessed=24 << 20, transcendentals=0

time: 133 us -> 129 us (0.970)
  Pallas kernels: 126 us -> 123 us
    pallas_call x1, Pallas kernels: 49.2 us -> 45.9 us  [gather(): pl.pallas_call(gather_kernel, in_specs=[hbm, hbm, vmem, hbm], out_specs=[...]
    unnamed x8 -> x18, local copies, waits for them, and re-layouts: 5.48 us -> 4.27 us
where the time goes in v4:
time: 129 us; the launch traced here: 128 us
  Pallas kernels  123 us (95%)
  local copies, waits for them, and re-layouts  4.27 us (3%)
    pallas_call x1, Pallas kernels, reduce(): pl.pallas_call(reduce_kernel, in_specs=[hbm, hbm, vmem, vmem, vmem, vmem,...  63.5 us
    pallas_call x1, Pallas kernels, gather(): pl.pallas_call(gather_kernel, in_specs=[hbm, hbm, vmem, hbm], out_specs=[...  45.9 us
    pallas_call x1, Pallas kernels, attention(): pl.pallas_call(attention_kernel, grid_spec=pltpu.PrefetchScalarGridSpec(n...  14.1 us
    unnamed x18, local copies, waits for them, and re-layouts  4.27 us

profile of v4, /device:TPU:0, one launch (start us, length us, event | category | flops | bytes accessed | tf_op | source)
XLA Modules:
  0.0 128.4 jit_solution(15887693202839883600)
XLA Ops:
  0.6 0.0 copy-start.5
  0.6 0.0 copy-start.4
  0.7 0.0 copy-start.3
  0.7 45.9 %gather.1 = (bf16[2,2048,512]{2,1,0:T(8,128)(2,1)}, bf16[16,2048,128]{2,1,0:T(8,128)(2,1)}, bf16[256,2048]{1,0:T(8,128)(2,1)}, bf16[256,2048]{1,0:T(8,128)(2,1)}) custom-call(bf16[256,512]{1,0:T(8,128)(2,1)} %bitcast.16, bf16[256,512]{1,0:T(8,128)(2,1)} %bitcast.17, bf16[256,2048]{1,0:T(8,128)(2,1)} %bitcast.9, bf16[2048,128]{1,0:T(8,128)(2,1)} %w.1), custom_call_target="tpu_custom_call" | custom-call | flops 2147483648 | bytes 25165824 | tf_op jit(solution)/shard_map/gather/pallas_call | solution.py:392
  46.6 0.0 copy-done.5
  46.6 0.0 copy-done.4
  46.6 0.0 copy-done.3
  46.6 0.0 copy-start.6
  46.6 1.2 copy-done.6
  47.9 0.0 copy-start
  47.9 0.0 copy-start.1
  47.9 0.0 copy-start.2
  47.9 14.1 %attention.1 = (bf16[256,2048]{1,0:T(8,128)(2,1)S(1)}, bf16[16,128,256]{2,1,0:T(8,128)(2,1)S(1)}, bf16[256,2048]{1,0:T(8,128)(2,1)}, bf16[2048,512]{1,0:T(8,128)(2,1)S(1)}, bf16[2048,512]{1,0:T(8,128)(2,1)S(1)}) custom-call(s32[2,8]{1,0:T(2,128)S(1)} %copy-done.4, s32[2]{0:T(128)S(1)} %copy-done.5, bf16[256,2048]{1,0:T(8,128)(2,1)S(1)} %bitcast.15, ...), custom_call_target="tpu_custom_call" | custom-call | flops 6442450944 | bytes 12582912 | tf_op jit(solution)/shard_map/attention/pallas_call | solution.py:124
  61.9 0.0 copy-done
  61.9 0.0 copy-done.1
  61.9 0.0 copy-done.2
  61.9 63.5 %reduce.1 = (bf16[256,2048]{1,0:T(8,128)(2,1)S(1)}, bf16[256,512]{1,0:T(8,128)(2,1)S(1)}, bf16[256,512]{1,0:T(8,128)(2,1)S(1)}, f32[256,128]{1,0:T(8,128)S(1)}) custom-call(bf16[2048,512]{1,0:T(8,128)(2,1)S(1)} %get-tuple-element.20.dk, bf16[2048,512]{1,0:T(8,128)(2,1)S(1)} %get-tuple-element.21.dv, bf16[256,2048]{1,0:T(8,128)(2,1)S(1)} %get-tuple-element.22.att, ...), custom_call_target="tpu_custom_call" | custom-call | flops 4294967296 | bytes 25165824 | tf_op jit(solution)/shard_map/reduce/pallas_call | solution.py:673
  125.4 1.0 copy.17
  126.4 0.7 copy.18
  127.1 0.7 copy.19
  127.8 0.7 copy.20
Async XLA Ops:
  0.6 46.0 %copy-start.5 = (s32[2]{0:T(128)S(1)}, s32[2]{0:T(128)}, u32[]{:S(2)}) copy-start(s32[2]{0:T(128)} %count_ref.1) | copy-start | bytes 28
  0.6 46.0 %copy-start.4 = (s32[2,8]{1,0:T(2,128)S(1)}, s32[2,8]{1,0:T(2,128)}, u32[]{:S(2)}) copy-start(s32[2,8]{1,0:T(2,128)} %list_ref.1) | copy-start | bytes 196
  0.7 46.0 %copy-start.3 = (bf16[1,256,2048]{2,1,0:T(8,128)(2,1)S(1)}, bf16[1,256,2048]{2,1,0:T(8,128)(2,1)}, u32[]{:S(2)}) copy-start(bf16[1,256,2048]{2,1,0:T(8,128)(2,1)} %param.8) | copy-start | bytes 3145732
  46.6 1.2 copy-start.6
  47.9 14.1 %copy-start = (bf16[1,256,2048]{2,1,0:T(8,128)(2,1)S(1)}, bf16[1,256,2048]{2,1,0:T(8,128)(2,1)}, u32[]{:S(2)}) copy-start(bf16[1,256,2048]{2,1,0:T(8,128)(2,1)} %param.12) | copy-start | bytes 3145732
  47.9 14.1 %copy-start.1 = (bf16[1,256,2048]{2,1,0:T(8,128)(2,1)S(1)}, bf16[1,256,2048]{2,1,0:T(8,128)(2,1)}, u32[]{:S(2)}) copy-start(bf16[1,256,2048]{2,1,0:T(8,128)(2,1)} %param.11) | copy-start | bytes 3145732
  47.9 14.1 %copy-start.2 = (bf16[256,2048]{1,0:T(8,128)(2,1)S(1)}, bf16[256,2048]{1,0:T(8,128)(2,1)}, u32[]{:S(2)}) copy-start(bf16[256,2048]{1,0:T(8,128)(2,1)} %get-tuple-element.24.grad_twin) | copy-start | bytes 3145732

commit v5 on v4

--- a/solution.py
+++ b/solution.py
@@ -220,7 +220,7 @@
             copy.wait_send()
 
 
-GATHER_FLOWS = 40
+GATHER_FLOWS = 41
 
 
 def gather_kernel(
@@ -253,6 +253,7 @@
     on_up = dict(gives=(z == 1) | (z == 2), takes=z >= 2)
     on_down = dict(gives=(z == 0) | (z == 3), takes=z >= 2)
     later = dict(gives=z >= 2, takes=z >= 2)
+    across = dict(gives=(z < 3) | (xh == 0), takes=(z < 3) | (xh == 1))
     w_side = [
         flows.send(w.at[pl.ds(p * half, half), :], part(f, p), at[("near", "back")[p]])
         for p in (0, 1)
@@ -261,7 +262,7 @@
     w_down = flows.send(w, whole(f), at["y_down"])
     kv_up = [flows.send(own[a], chunk(a, c), at["z_up"], **up) for a in (0, 1)]
     kv_down = [flows.send(own[a], chunk(a, c), at["z_down"], **down[a]) for a in (1, 0)][::-1]
-    kv_far = [flows.send(own[a], chunk(a, c), at["far"]) for a in (0, 1)]
+    kv_far = [flows.send(own[a], chunk(a, c), at["far"], **across) for a in (0, 1)]
     to_twin = [flows.send(w, whole(f), at["twin"])]
     swap = flows.send(grad, grad_twin, at["twin"])
     here = [
@@ -354,23 +355,23 @@
     got = 2 * z_up + 1 - xh
     pair_on_v = flows.send(piece(1, got, 0), piece(1, got, 0), at["z_down"], **on_down)
 
-    for yy, arrived in ((y_down, side_up), (y_up, side_down)):
-        got = shard(yy, 1 - xl, k)
-        for copy in arrived:
-            copy.wait_recv()
-        to_twin.append(flows.send(whole(got), whole(got), at["twin"]))
+    for p in (0, 1):
+        for yy, arrived in ((y_down, side_up), (y_up, side_down)):
+            got = shard(yy, 1 - xl, k)
+            arrived[p].wait_recv()
+            to_twin.append(flows.send(part(got, p), part(got, p), at["twin"]))
     got = shard(y_far, 1 - xl, k)
     on_s0.wait_recv()
     to_twin.append(flows.send(part(got, 0), part(got, 0), at["twin"]))
     on_s1.wait_recv()
     to_twin.append(flows.send(part(got, 1), part(got, 1), at["twin"]))
-    for n in (1, 6):
+    for n in (1, 6, 8):
         to_twin[n].wait_recv()
     multiply(y_down, 1)
-    for n in (2, 7):
+    for n in (2, 7, 9):
         to_twin[n].wait_recv()
     multiply(y_up, 2)
-    for n in (4, 5, 8, 9):
+    for n in (4, 5, 10, 11):
         to_twin[n].wait_recv()
     multiply(y_far, 3)
     datt[...] = total[...].astype(BF16)
@@ -451,6 +452,7 @@
     hop_in_k, hop_in_v = z_down >= 2, z_up >= 2
     raw_in_k, raw_in_v = z_up >= 1, z_down == 3
     sum_in_k, sum_in_v = (z_down == 3) | (z_down == 0), z_up >= 1
+    far_gives, far_takes = (z < 3) | (xh == 1), (z < 3) | (xh == 0)
     for buffer, a, comes in (
         (hop_in, 0, hop_in_k),
         (hop_in, 1, hop_in_v),
@@ -458,6 +460,8 @@
         (raw_in, 1, raw_in_v),
         (sum_in, 0, sum_in_k),
         (sum_in, 1, sum_in_v),
+        (far_in, 0, far_takes),
+        (far_in, 1, far_takes),
     ):
 
         def clear(buffer=buffer, a=a):
@@ -588,7 +592,9 @@
                 )
 
             far_out[a, p] = gathered(give_rows).astype(BF16)
-            fars[p].append(flows.send(far_out.at[a, p], far_in.at[a, p], at["far"]))
+            fars[p].append(
+                flows.send(far_out.at[a, p], far_in.at[a, p], at["far"], far_gives, far_takes)
+            )
             kept[a, p] = gathered(keep_rows)
 
     def cross(p):

time: 129 us -> 129 us (level)
  no operation moved by 1% of the time
where the time goes in v5:
time: 129 us; the launch traced here: 128 us
  Pallas kernels  123 us (95%)
  local copies, waits for them, and re-layouts  4.27 us (3%)
    pallas_call x1, Pallas kernels, reduce(): pl.pallas_call(reduce_kernel, in_specs=[hbm, hbm, vmem, vmem, vmem, vmem,...  63.2 us
    pallas_call x1, Pallas kernels, gather(): pl.pallas_call(gather_kernel, in_specs=[hbm, hbm, vmem, hbm], out_specs=[...  46 us
    pallas_call x1, Pallas kernels, attention(): pl.pallas_call(attention_kernel, grid_spec=pltpu.PrefetchScalarGridSpec(n...  14.1 us
    unnamed x18, local copies, waits for them, and re-layouts  4.27 us

profile of v5, /device:TPU:0, one launch (start us, length us, event | category | flops | bytes accessed | tf_op | source)
XLA Modules:
  0.0 128.2 jit_solution(4798147667442235325)
XLA Ops:
  0.6 0.0 copy-start.5
  0.6 0.0 copy-start.4
  0.7 0.0 copy-start.3
  0.7 46.0 %gather.1 = (bf16[2,2048,512]{2,1,0:T(8,128)(2,1)}, bf16[16,2048,128]{2,1,0:T(8,128)(2,1)}, bf16[256,2048]{1,0:T(8,128)(2,1)}, bf16[256,2048]{1,0:T(8,128)(2,1)}) custom-call(bf16[256,512]{1,0:T(8,128)(2,1)} %bitcast.16, bf16[256,512]{1,0:T(8,128)(2,1)} %bitcast.17, bf16[256,2048]{1,0:T(8,128)(2,1)} %bitcast.9, bf16[2048,128]{1,0:T(8,128)(2,1)} %w.1), custom_call_target="tpu_custom_call" | custom-call | flops 2147483648 | bytes 25165824 | tf_op jit(solution)/shard_map/gather/pallas_call | solution.py:393
  46.6 0.0 copy-done.5
  46.6 0.0 copy-done.4
  46.7 0.0 copy-done.3
  46.7 0.0 copy-start.6
  46.7 1.2 copy-done.6
  47.9 0.0 copy-start
  47.9 0.0 copy-start.1
  47.9 0.0 copy-start.2
  47.9 14.1 %attention.1 = (bf16[256,2048]{1,0:T(8,128)(2,1)S(1)}, bf16[16,128,256]{2,1,0:T(8,128)(2,1)S(1)}, bf16[256,2048]{1,0:T(8,128)(2,1)}, bf16[2048,512]{1,0:T(8,128)(2,1)S(1)}, bf16[2048,512]{1,0:T(8,128)(2,1)S(1)}) custom-call(s32[2,8]{1,0:T(2,128)S(1)} %copy-done.4, s32[2]{0:T(128)S(1)} %copy-done.5, bf16[256,2048]{1,0:T(8,128)(2,1)S(1)} %bitcast.15, ...), custom_call_target="tpu_custom_call" | custom-call | flops 6442450944 | bytes 12582912 | tf_op jit(solution)/shard_map/attention/pallas_call | solution.py:124
  62.0 0.0 copy-done
  62.0 0.0 copy-done.1
  62.0 0.0 copy-done.2
  62.0 63.2 %reduce.1 = (bf16[256,2048]{1,0:T(8,128)(2,1)S(1)}, bf16[256,512]{1,0:T(8,128)(2,1)S(1)}, bf16[256,512]{1,0:T(8,128)(2,1)S(1)}, f32[256,128]{1,0:T(8,128)S(1)}) custom-call(bf16[2048,512]{1,0:T(8,128)(2,1)S(1)} %get-tuple-element.20.dk, bf16[2048,512]{1,0:T(8,128)(2,1)S(1)} %get-tuple-element.21.dv, bf16[256,2048]{1,0:T(8,128)(2,1)S(1)} %get-tuple-element.22.att, ...), custom_call_target="tpu_custom_call" | custom-call | flops 4294967296 | bytes 25165824 | tf_op jit(solution)/shard_map/reduce/pallas_call | solution.py:679
  125.2 1.0 copy.17
  126.2 0.7 copy.18
  126.9 0.7 copy.19
  127.6 0.7 copy.20
Async XLA Ops:
  0.6 46.0 %copy-start.5 = (s32[2]{0:T(128)S(1)}, s32[2]{0:T(128)}, u32[]{:S(2)}) copy-start(s32[2]{0:T(128)} %count_ref.1) | copy-start | bytes 28
  0.6 46.0 %copy-start.4 = (s32[2,8]{1,0:T(2,128)S(1)}, s32[2,8]{1,0:T(2,128)}, u32[]{:S(2)}) copy-start(s32[2,8]{1,0:T(2,128)} %list_ref.1) | copy-start | bytes 196
  0.7 46.0 %copy-start.3 = (bf16[1,256,2048]{2,1,0:T(8,128)(2,1)S(1)}, bf16[1,256,2048]{2,1,0:T(8,128)(2,1)}, u32[]{:S(2)}) copy-start(bf16[1,256,2048]{2,1,0:T(8,128)(2,1)} %param.8) | copy-start | bytes 3145732
  46.7 1.2 copy-start.6
  47.9 14.1 %copy-start = (bf16[1,256,2048]{2,1,0:T(8,128)(2,1)S(1)}, bf16[1,256,2048]{2,1,0:T(8,128)(2,1)}, u32[]{:S(2)}) copy-start(bf16[1,256,2048]{2,1,0:T(8,128)(2,1)} %param.12) | copy-start | bytes 3145732
  47.9 14.1 %copy-start.1 = (bf16[1,256,2048]{2,1,0:T(8,128)(2,1)S(1)}, bf16[1,256,2048]{2,1,0:T(8,128)(2,1)}, u32[]{:S(2)}) copy-start(bf16[1,256,2048]{2,1,0:T(8,128)(2,1)} %param.11) | copy-start | bytes 3145732
  47.9 14.1 %copy-start.2 = (bf16[256,2048]{1,0:T(8,128)(2,1)S(1)}, bf16[256,2048]{1,0:T(8,128)(2,1)}, u32[]{:S(2)}) copy-start(bf16[256,2048]{1,0:T(8,128)(2,1)} %get-tuple-element.24.grad_twin) | copy-start | bytes 3145732

commit v6 on v4

--- a/solution.py
+++ b/solution.py
@@ -447,7 +447,10 @@
             pl.ds(pl.multiple_of(zz * pair, pair), pair), pl.ds(p * wide, wide)
         ]
 
-    swap = flows.send(att_t, att_twin, at["twin"])
+    stripes = [pl.ds(n * PART_ROWS, PART_ROWS) for n in range(PARTS // 2)]
+    swaps = [
+        flows.send(att_t.at[:, s, :], att_twin.at[:, s, :], at["twin"]) for s in stripes
+    ]
     hop_in_k, hop_in_v = z_down >= 2, z_up >= 2
     raw_in_k, raw_in_v = z_up >= 1, z_down == 3
     sum_in_k, sum_in_v = (z_down == 3) | (z_down == 0), z_up >= 1
@@ -483,7 +486,8 @@
         ]
     ):
         copy = pltpu.make_async_copy(src, dst, here_sem.at[n])
-        copy.start()
+        if n < 4:
+            copy.start()
         here.append(copy)
 
     def product(yy, p, low):
@@ -501,9 +505,10 @@
         out = term(att_t, grad) + term(att_twin, grad_twin)
         return out.reshape(4, PART_ROWS, 2 * HEAD_DIM)
 
-    swap.wait_recv()
     top_hop, low_hop = [], []
     for p in range(PARTS):
+        if p < len(swaps):
+            swaps[p].wait_recv()
         far_p[p, 0:4] = product(y_far, p, 0).astype(BF16)
         top_hop.append(flows.send(far_p.at[p, pl.ds(0, 4)], top_in.at[p], at["y_up"]))
         far_p[p, 4:8] = product(y_far, p, 4).astype(BF16)
@@ -547,6 +552,7 @@
         low_on.append(flows.send(low_out.at[p], low_sum.at[p], at["y_down"]))
         if p % 2:
             relay_kv(p // 2)
+            here[4 + p // 2].start()
     for p in range(PARTS):
         own_keep[p, 0:4] = product(y, p, 0)
         own_keep[p, 4:8] = product(y, p, 4)

time: 129 us -> 128 us (level)
  no operation moved by 1% of the time
where the time goes in v6:
time: 128 us
  Pallas kernels  123 us (96%)
  local copies, waits for them, and re-layouts  4.27 us (3%)
    pallas_call x1, Pallas kernels, reduce(): pl.pallas_call(reduce_kernel, in_specs=[hbm, hbm, vmem, vmem, vmem, vmem,...  62.7 us
    pallas_call x1, Pallas kernels, gather(): pl.pallas_call(gather_kernel, in_specs=[hbm, hbm, vmem, hbm], out_specs=[...  45.9 us
    pallas_call x1, Pallas kernels, attention(): pl.pallas_call(attention_kernel, grid_spec=pltpu.PrefetchScalarGridSpec(n...  14.1 us
    unnamed x18, local copies, waits for them, and re-layouts  4.27 us

profile of v6, /device:TPU:0, one launch (start us, length us, event | category | flops | bytes accessed | tf_op | source)
XLA Modules:
  0.0 127.7 jit_solution(8312396976676309838)
XLA Ops:
  0.6 0.0 copy-start.5
  0.6 0.0 copy-start.4
  0.7 0.0 copy-start.3
  0.7 45.9 %gather.1 = (bf16[2,2048,512]{2,1,0:T(8,128)(2,1)}, bf16[16,2048,128]{2,1,0:T(8,128)(2,1)}, bf16[256,2048]{1,0:T(8,128)(2,1)}, bf16[256,2048]{1,0:T(8,128)(2,1)}) custom-call(bf16[256,512]{1,0:T(8,128)(2,1)} %bitcast.16, bf16[256,512]{1,0:T(8,128)(2,1)} %bitcast.17, bf16[256,2048]{1,0:T(8,128)(2,1)} %bitcast.9, bf16[2048,128]{1,0:T(8,128)(2,1)} %w.1), custom_call_target="tpu_custom_call" | custom-call | flops 2147483648 | bytes 25165824 | tf_op jit(solution)/shard_map/gather/pallas_call | solution.py:392
  46.6 0.0 copy-done.5
  46.6 0.0 copy-done.4
  46.6 0.0 copy-done.3
  46.6 0.0 copy-start.6
  46.6 1.2 copy-done.6
  47.9 0.0 copy-start
  47.9 0.0 copy-start.1
  47.9 0.0 copy-start.2
  47.9 14.1 %attention.1 = (bf16[256,2048]{1,0:T(8,128)(2,1)S(1)}, bf16[16,128,256]{2,1,0:T(8,128)(2,1)S(1)}, bf16[256,2048]{1,0:T(8,128)(2,1)}, bf16[2048,512]{1,0:T(8,128)(2,1)S(1)}, bf16[2048,512]{1,0:T(8,128)(2,1)S(1)}) custom-call(s32[2,8]{1,0:T(2,128)S(1)} %copy-done.4, s32[2]{0:T(128)S(1)} %copy-done.5, bf16[256,2048]{1,0:T(8,128)(2,1)S(1)} %bitcast.15, ...), custom_call_target="tpu_custom_call" | custom-call | flops 6442450944 | bytes 12582912 | tf_op jit(solution)/shard_map/attention/pallas_call | solution.py:124
  61.9 0.0 copy-done
  61.9 0.0 copy-done.1
  61.9 0.0 copy-done.2
  61.9 62.7 %reduce.1 = (bf16[256,2048]{1,0:T(8,128)(2,1)S(1)}, bf16[256,512]{1,0:T(8,128)(2,1)S(1)}, bf16[256,512]{1,0:T(8,128)(2,1)S(1)}, f32[256,128]{1,0:T(8,128)S(1)}) custom-call(bf16[2048,512]{1,0:T(8,128)(2,1)S(1)} %get-tuple-element.20.dk, bf16[2048,512]{1,0:T(8,128)(2,1)S(1)} %get-tuple-element.21.dv, bf16[256,2048]{1,0:T(8,128)(2,1)S(1)} %get-tuple-element.22.att, ...), custom_call_target="tpu_custom_call" | custom-call | flops 4294967296 | bytes 25165824 | tf_op jit(solution)/shard_map/reduce/pallas_call | solution.py:679
  124.7 1.0 copy.17
  125.6 0.7 copy.18
  126.3 0.7 copy.19
  127.0 0.7 copy.20
Async XLA Ops:
  0.6 46.0 %copy-start.5 = (s32[2]{0:T(128)S(1)}, s32[2]{0:T(128)}, u32[]{:S(2)}) copy-start(s32[2]{0:T(128)} %count_ref.1) | copy-start | bytes 28
  0.6 46.0 %copy-start.4 = (s32[2,8]{1,0:T(2,128)S(1)}, s32[2,8]{1,0:T(2,128)}, u32[]{:S(2)}) copy-start(s32[2,8]{1,0:T(2,128)} %list_ref.1) | copy-start | bytes 196
  0.7 46.0 %copy-start.3 = (bf16[1,256,2048]{2,1,0:T(8,128)(2,1)S(1)}, bf16[1,256,2048]{2,1,0:T(8,128)(2,1)}, u32[]{:S(2)}) copy-start(bf16[1,256,2048]{2,1,0:T(8,128)(2,1)} %param.8) | copy-start | bytes 3145732
  46.6 1.2 copy-start.6
  47.9 14.1 %copy-start = (bf16[1,256,2048]{2,1,0:T(8,128)(2,1)S(1)}, bf16[1,256,2048]{2,1,0:T(8,128)(2,1)}, u32[]{:S(2)}) copy-start(bf16[1,256,2048]{2,1,0:T(8,128)(2,1)} %param.12) | copy-start | bytes 3145732
  47.9 14.1 %copy-start.1 = (bf16[1,256,2048]{2,1,0:T(8,128)(2,1)S(1)}, bf16[1,256,2048]{2,1,0:T(8,128)(2,1)}, u32[]{:S(2)}) copy-start(bf16[1,256,2048]{2,1,0:T(8,128)(2,1)} %param.11) | copy-start | bytes 3145732
  47.9 14.1 %copy-start.2 = (bf16[256,2048]{1,0:T(8,128)(2,1)S(1)}, bf16[256,2048]{1,0:T(8,128)(2,1)}, u32[]{:S(2)}) copy-start(bf16[256,2048]{1,0:T(8,128)(2,1)} %get-tuple-element.24.grad_twin) | copy-start | bytes 3145732
